TPU v7x, 256 devices: a whole 4x4x8 slice. The times are simulated.
256 devices in a mesh: seq: 16 (over z, x_hi), res: 16 (over x_lo, y, core).
Axes of the slice: x: 4 (x_hi: 2, x_lo: 2; x = x_hi * 2 + x_lo), y: 4, z: 8, core: 2. Of those that a mesh axis runs over, the one named last changes fastest.
Arguments:
- alignment: bfloat16 [256, 1024, 256], P('res', 'seq'), may hold values from -6 to 6
- alignment_mask: int32 [256, 1024], P('res', 'seq'), may hold values from 0 to 1, as said below
- residue_mask: int32 [1024], replicated, may hold values from 0 to 1, as said below
- pair_input: float32 [1024, 1024, 128], P('seq', 'res'), may hold values from -6 to 6
- outer_gain: float32 [256], replicated, may hold values from 0.25 to 1.75
- left_weight: bfloat16 [256, 32], replicated, may hold values from -0.375 to 0.375
- right_weight: bfloat16 [256, 32], replicated, may hold values from -0.375 to 0.375
- outer_weight: bfloat16 [1024, 128], replicated, may hold values from -1 to 1
- pair_gain: float32 [128], replicated, may hold values from 0.25 to 1.75
- bias_weight: bfloat16 [128, 8], replicated, may hold values from -48 to 48
- row_gain: float32 [256], replicated, may hold values from 0.25 to 1.75
- query_weight: bfloat16 [256, 256], replicated, may hold values from -0.375 to 0.375
- key_weight: bfloat16 [256, 256], replicated, may hold values from -0.375 to 0.375
- value_weight: bfloat16 [256, 256], replicated, may hold values from -0.375 to 0.375
- gate_weight: bfloat16 [256, 256], replicated, may hold values from -0.375 to 0.375
- output_weight: bfloat16 [256, 256], replicated, may hold values from -2 to 2
- transition_gain: float32 [256], replicated, may hold values from 0.25 to 1.75
- up_weight: bfloat16 [256, 1024], replicated, may hold values from -0.375 to 0.375
- down_weight: bfloat16 [1024, 256], replicated, may hold values from -0.1875 to 0.1875
Outputs:
- pair_output: float32 [1024, 1024, 128], P('seq', 'res')
- alignment_output: float32 [256, 1024, 256], P('res', 'seq')
Inputs may be any that keep to these rules, and one draw needn't show every extreme that they name: `residue_mask`: 1 for a present residue, 0 for padding; at least one residue is 1 and at least one is 0. Some residue whose residue_mask is 1 has alignment_mask 1 in every sequence.
All inputs are finite; a program needn't handle non-finite values.
Results may differ from a plain program's by a relative error of at most 0.04.
Values may be sent and summed in bfloat16 or wider, within the bound.
A program may use at most 128 MiB of HBM per device.

v0:
```python
import math

import jax
import jax.numpy as jnp
from jax import lax
from jax.sharding import PartitionSpec as P

EPSILON = 1e-05
MASKED = -1000000000.0
SCORE_LIMIT = 524288


def sent_together(arrays, axis, dim, along):
    columns = [a.reshape(*a.shape[:along], -1) for a in arrays]
    both = jnp.concatenate(columns, axis=along)
    result, at, finished = (lax.all_gather(both, axis, axis=dim, tiled=True), 0, [])
    for a, column in zip(arrays, columns):
        piece = result[..., at : at + column.shape[along]]
        finished.append(piece.reshape(*piece.shape[:along], *a.shape[along:]))
        at += column.shape[along]
    return tuple(finished)


def sent_together_2(arrays, axis, split_dim, concat_dim, along):
    columns = [a.reshape(*a.shape[:along], -1) for a in arrays]
    both = jnp.concatenate(columns, axis=along)
    result, at, finished = (
        lax.all_to_all(both, axis, split_axis=split_dim, concat_axis=concat_dim, tiled=True),
        0,
        [],
    )
    for a, column in zip(arrays, columns):
        piece = result[..., at : at + column.shape[along]]
        finished.append(piece.reshape(*piece.shape[:along], *a.shape[along:]))
        at += column.shape[along]
    return tuple(finished)


def copy_for_each(x, axis):
    copies = jnp.broadcast_to(x, (lax.axis_size(axis), *x.shape))
    return lax.all_to_all(copies, axis, split_axis=0, concat_axis=0, tiled=True)


def laid_out(blocks, dim):
    blocks = jnp.moveaxis(blocks, 0, dim)
    lengths = blocks.shape
    return blocks.reshape(*lengths[:dim], lengths[dim] * lengths[dim + 1], *lengths[dim + 2 :])


def gather_directly(x, axis, dim):
    blocks = copy_for_each(x, axis)
    return laid_out(blocks, dim)


def layer_norm(values, scales):
    values = values.astype(jnp.float32)
    center = values - jnp.mean(values, -1, keepdims=True)
    spread = jnp.mean(center * center, -1, keepdims=True)
    return center * lax.rsqrt(spread + EPSILON) * scales


def project(values, weight):
    flattened = values.reshape(-1, values.shape[-1])
    result = jnp.dot(flattened, weight, preferred_element_type=jnp.float32)
    return result.reshape(values.shape[:-1] + (weight.shape[1],))


def block_size(length, per_item):
    item_limit = max(1, SCORE_LIMIT // per_item)
    return max(
        (
            divisor
            for divisor in range(1, length + 1)
            if length % divisor == 0 and divisor <= item_limit
        )
    )


def in_blocks(function, arrays, block_rows):
    shaped = tuple(
        (
            member.reshape((member.shape[0] // block_rows, block_rows) + member.shape[1:])
            for member in arrays
        )
    )
    outputs = lax.map(function, shaped)
    return jax.tree.map(lambda member: member.reshape((-1,) + member.shape[2:]), outputs)


def head_scores(query_rows, key_rows, live_keys, head_bias, head_count, score_scale):
    seq_block, row_count, features = query_rows.shape
    key_count = key_rows.shape[1]
    head_size = features // head_count
    scores = jnp.einsum(
        "sihd,sjhd->shij",
        query_rows.reshape(seq_block, row_count, head_count, head_size),
        key_rows.reshape(seq_block, key_count, head_count, head_size),
        preferred_element_type=jnp.float32,
    )
    scores = scores * score_scale + head_bias.astype(jnp.float32)[None]
    return jnp.where(live_keys[:, None, None, :] > 0, scores, MASKED)


def head_weigh(scores, score_peaks, values, head_count):
    weights = jnp.exp(scores - score_peaks[..., None])
    totals = jnp.swapaxes(jnp.sum(weights, -1), 1, 2)
    seq_block, key_count, features = values.shape
    mixed_sum = jnp.einsum(
        "shij,sjhd->sihd",
        weights.astype(jnp.bfloat16),
        values.reshape(seq_block, key_count, head_count, features // head_count),
        preferred_element_type=jnp.float32,
    )
    return (mixed_sum.reshape(seq_block, mixed_sum.shape[1], features), totals)


def on_device(
    alignment,
    alignment_mask,
    residue_mask,
    pair_input,
    outer_gain,
    left_weight,
    right_weight,
    outer_weight,
    pair_gain,
    bias_weight,
    row_gain,
    query_weight,
    key_weight,
    value_weight,
    gate_weight,
    output_weight,
    transition_gain,
    up_weight,
    down_weight,
):
    seq_share, row_count = (alignment.shape[0], alignment.shape[1])
    res_local = pair_input.shape[1]
    seq_total = seq_share * lax.axis_size("res")
    res_total = row_count * lax.axis_size("seq")
    head_count = bias_weight.shape[1]
    outer_width = left_weight.shape[1]
    pair_width = pair_input.shape[2]
    score_scale = (query_weight.shape[1] // head_count) ** (-0.5)
    residue_live = residue_mask.astype(jnp.float32)
    row_live = lax.dynamic_slice_in_dim(residue_live, lax.axis_index("seq") * row_count, row_count)
    column_live = lax.dynamic_slice_in_dim(
        residue_live, lax.axis_index("res") * res_local, res_local
    )
    mask_local = alignment_mask.astype(jnp.bfloat16)
    own_live = alignment_mask.astype(jnp.float32) * row_live[None, :]
    outer_norm = layer_norm(alignment, outer_gain).astype(jnp.bfloat16)
    row_norm = layer_norm(alignment, row_gain).astype(jnp.bfloat16)
    left_local = (project(outer_norm, left_weight) * own_live[..., None]).astype(jnp.bfloat16)
    left_proj, row_mask = sent_together((left_local, mask_local), "res", 0, 2)
    row_flags = (row_mask.astype(jnp.float32) * row_live[None, :]).astype(jnp.bfloat16)
    wide_alignment, wide_mask = (
        lax.all_gather(alignment, "seq", axis=1, tiled=True),
        lax.all_gather(mask_local, "seq", axis=1, tiled=True),
    )
    wide_live = wide_mask.astype(jnp.float32) * residue_live[None, :]
    key_norm = layer_norm(wide_alignment, row_gain).astype(jnp.bfloat16)
    outer_wide = layer_norm(wide_alignment, outer_gain).astype(jnp.bfloat16)
    all_keys = project(key_norm, key_weight).astype(jnp.bfloat16)
    all_values = project(key_norm, value_weight).astype(jnp.bfloat16)
    wide_right = (project(outer_wide, right_weight) * wide_live[..., None]).astype(jnp.bfloat16)
    right_proj, column_mask = sent_together_2((wide_right, wide_mask), "res", 1, 0, 2)
    column_flags = (column_mask.astype(jnp.float32) * column_live[None, :]).astype(jnp.bfloat16)
    right_flat = right_proj.reshape(seq_total, res_local * outer_width)
    row_step = math.gcd(row_count, 16)

    def outer_rows(row_start):
        left_piece = lax.dynamic_slice_in_dim(left_proj, row_start, row_step, 1).reshape(
            seq_total, row_step * outer_width
        )
        product = lax.dot_general(
            left_piece, right_flat, (((0,), (0,)), ((), ())), preferred_element_type=jnp.float32
        )
        product = product.reshape(row_step, outer_width, res_local, outer_width).transpose(
            0, 2, 1, 3
        )
        product = product.reshape(row_step * res_local, outer_width * outer_width).astype(
            jnp.bfloat16
        )
        update = jnp.dot(product, outer_weight, preferred_element_type=jnp.float32).reshape(
            row_step, res_local, pair_width
        )
        live_rows = lax.dynamic_slice_in_dim(row_flags, row_start, row_step, 1)
        counts = lax.dot_general(
            live_rows, column_flags, (((0,), (0,)), ((), ())), preferred_element_type=jnp.float32
        )
        return update / jnp.maximum(counts, 1.0)[..., None]

    starts = jnp.arange(row_count // row_step, dtype=jnp.int32) * row_step
    outer_update = lax.map(outer_rows, starts).reshape(row_count, res_local, pair_width)
    pair_output = pair_input + outer_update
    pair_norm = layer_norm(pair_output, pair_gain).astype(jnp.bfloat16)
    pair_bias = jnp.einsum(
        "ijc,ch->hij", pair_norm, bias_weight, preferred_element_type=jnp.float32
    ).astype(jnp.bfloat16)
    full_bias = gather_directly(pair_bias, "res", 2)
    own_queries = project(row_norm, query_weight).astype(jnp.bfloat16)
    gate_values = jax.nn.sigmoid(project(row_norm, gate_weight))
    seq_step = block_size(seq_share, head_count * row_count * res_total)

    def attend_piece(members):
        query_piece, key_piece, value_piece, live_piece = members
        scores = head_scores(query_piece, key_piece, live_piece, full_bias, head_count, score_scale)
        return head_weigh(scores, jnp.max(scores, -1), value_piece, head_count)

    mixed_sum, totals = in_blocks(
        attend_piece, (own_queries, all_keys, all_values, wide_live), seq_step
    )
    attended = (
        mixed_sum.reshape(seq_share, row_count, head_count, -1) / totals[..., None]
    ).reshape(seq_share, row_count, -1)
    gated_rows = (attended * gate_values).astype(jnp.bfloat16)
    after_rows = alignment.astype(jnp.float32) + project(gated_rows, output_weight)
    trans_norm = layer_norm(after_rows, transition_gain).astype(jnp.bfloat16)
    hidden_units = jnp.maximum(project(trans_norm, up_weight), 0.0).astype(jnp.bfloat16)
    alignment_output = after_rows + project(hidden_units, down_weight)
    return (pair_output, alignment_output)


def solution(mesh):
    in_specs = (
        P("res", "seq", None),
        P("res", "seq"),
        P(),
        P("seq", "res", None),
        P(),
        P(),
        P(),
        P(),
        P(),
        P(),
        P(),
        P(),
        P(),
        P(),
        P(),
        P(),
        P(),
        P(),
        P(),
    )
    out_specs = (P("seq", "res", None), P("res", "seq", None))
    return jax.shard_map(
        on_device, mesh=mesh, in_specs=in_specs, out_specs=out_specs, check_vma=False
    )
```

profile of v0, /device:TPU:1, one launch (start us, length us, event | category | flops | bytes accessed | tf_op | source)
XLA Modules:
  0.0 468.4 jit_solution(8661635118987112832)
XLA Ops:
  15.2 38.0 %all-gather = bf16[16,64,16]{1,2,0:T(8,128)(2,1)S(1)} all-gather(bf16[1,64,16]{1,2,0:T(8,128)(2,1)S(1)} %get-tuple-element.226), channel_id=1, replica_groups=mesh['seq'=16,'res'=16] {'seq'}, dimensions={0}, use_global_device_ids=true | all-gather | bytes 34816 | tf_op jit(solution)/shard_map/all_gather | solution.py:160
  53.4 96.5 %all-gather.6.cloned.1.call-done = bf16[16,1024,256]{2,1,0:T(8,128)(2,1)} async-done(((bf16[16,64,256]{2,1,0:T(8,128)(2,1)}), bf16[16,1024,256]{2,1,0:T(8,128)(2,1)}) %all-gather.6.cloned.1.call-update) | async-done | bytes 8388624 | tf_op jit(solution)/shard_map/all_gather | solution.py:159
  149.9 5.8 %convert_reduce_fusion = f32[16,1024]{1,0:T(8,128)S(1)} fusion(bf16[16,1024,256]{2,1,0:T(8,128)(2,1)} %all-gather.6.cloned.1.call-done), kind=kLoop, calls=%fused_computation.26 | loop fusion | flops 8372224 | bytes 8454144 | tf_op jit(solution)/shard_map/reduce_sum | solution.py:57
  155.7 4.8 %fusion.21 = f32[16,1024]{1,0:T(8,128)S(1)} fusion(bf16[16,1024,256]{2,1,0:T(8,128)(2,1)S(1)} %copy-done.1, f32[16,1024]{1,0:T(8,128)S(1)} %broadcast_multiply_fusion), kind=kLoop, calls=%fused_computation.33 | loop fusion | flops 16760832 | bytes 8519680 | tf_op jit(solution)/shard_map/reduce_sum | solution.py:58
  160.6 7.6 %multiply_convert_fusion.1 = bf16[16,1024,32]{1,2,0:T(8,128)(2,1)S(1)} fusion(bf16[16,1024,256]{2,1,0:T(8,128)(2,1)S(1)} %copy-done.1, f32[256]{0:T(256)S(1)} %copy-done.15, f32[16,1024]{1,0:T(8,128)S(1)} %add_rsqrt_fusion, f32[16,1024]{1,0:T(8,128)S(1)} %broadcast_multiply_fusion, f32[16,1024]{1,0:T(8,128)S(1)} %get-tuple-element.225, ...), kind=kOutput, calls=%fused_computation.43 | convolution fusion | flops 290455552 | bytes 9651200 | tf_op jit(solution)/shard_map/dot_general | solution.py:64
  168.4 5.0 %copy.105 = bf16[16,1024,33]{2,0,1:T(8,128)(2,1)} copy(bf16[16,1024,33]{1,2,0:T(8,128)(2,1)S(1)} %pad_maximum_fusion) | data formatting | bytes 2162688 | tf_op jit(solution)/shard_map/concatenate | solution.py:26
  173.4 9.5 %reshape.221 = bf16[16,2,16896]{2,1,0:T(2,128)(2,1)} reshape(bf16[1024,16,33]{2,1,0:T(8,128)(2,1)} %bitcast.184) | data formatting | bytes 2162688
  182.8 5.4 %all-to-all-start = ((bf16[16,2,16896]{2,1,0:T(2,128)(2,1)}), bf16[16,2,16896]{2,1,0:T(2,128)(2,1)}, u32[]{:S(2)}, u32[]{:S(2)}) async-start(bf16[16,2,16896]{2,1,0:T(2,128)(2,1)} %reshape.221), calls=%async_computation | async-start | bytes 2162688 | tf_op jit(solution)/shard_map/all_to_all | solution.py:28
  194.8 9.8 %all-to-all-done = bf16[16,2,16896]{2,1,0:T(2,128)(2,1)} async-done(((bf16[16,2,16896]{2,1,0:T(2,128)(2,1)}), bf16[16,2,16896]{2,1,0:T(2,128)(2,1)}, u32[]{:S(2)}, u32[]{:S(2)}) %all-to-all-start) | async-done | bytes 1081376 | tf_op jit(solution)/shard_map/all_to_all | solution.py:28
  204.6 12.6 %reshape.222 = bf16[1024,16,33]{2,1,0:T(8,128)(2,1)} reshape(bf16[16,2,16896]{2,1,0:T(2,128)(2,1)} %all-to-all-done) | data formatting | bytes 2162688
  217.2 7.1 %copy.107 = bf16[16,16,64,33]{2,1,0,3:T(8,128)(2,1)S(1)} copy(bf16[16,16,64,33]{3,1,2,0:T(8,128)(2,1)} %bitcast.183) | data formatting | bytes 2162688 | tf_op jit(solution)/shard_map/all_to_all | solution.py:28
  228.6 38.7 %while.22 = (s32[]{:T(128)}, f32[4,16,64,128]{3,2,1,0:T(8,128)}, s32[4]{0:T(128)S(1)}, bf16[256,64,32]{0,2,1:T(8,128)(2,1)}, bf16[256,2048]{0,1:T(8,128)(2,1)S(1...) while((s32[]{:T(128)}, f32[4,16,64,128]{3,2,1,0:T(8,128)}, ...), condition=%wide.region_5.0_spmd, body=%wide.region_4.0_spmd.sunk | while | flops 807011328 | bytes 11608767 | solution.py:196
  231.1 3.0 convert_bitcast_fusion.6
  240.8 3.0 convert_bitcast_fusion.6
  250.4 3.0 convert_bitcast_fusion.6
  260.1 3.0 convert_bitcast_fusion.6
  267.3 2.9 fusion.91
  276.1 5.0 %all-to-all-start.1 = ((bf16[16,2,16384]{2,1,0:T(2,128)(2,1)}), bf16[16,2,16384]{2,1,0:T(2,128)(2,1)}, u32[]{:S(2)}, u32[]{:S(2)}) async-start(bf16[16,2,16384]{2,1,0:T(2,128)(2,1)} %reshape.223), calls=%async_computation.1 | async-start | bytes 2097152 | tf_op jit(solution)/shard_map/all_to_all | solution.py:41
  281.1 9.4 %convert_bitcast_fusion.1 = bf16[16,1,1024,256]{3,2,0,1:T(8,128)(2,1)} fusion(bf16[16,1024,256]{2,1,0:T(8,128)(2,1)} %all-gather.6.cloned.1.call-done, f32[256]{0:T(256)S(1)} %copy-done.16, f32[16,1024]{1,0:T(8,128)S(1)} %add_rsqrt_fusion, f32[16,1024]{1,0:T(8,128)S(1)} %broadcast_multiply_fusion, bf16[256,256]{1,0:T(8,128)(2,1)S(1)} %copy-done.10), kind=kOutput, calls=%fused_computation.35 | convolution fusion | flops 2172649472 | bytes 17040384 | tf_op jit(solution)/shard_map/dot_general | solution.py:64
  290.4 9.3 %convert_bitcast_fusion.2 = bf16[16,1,1024,256]{3,2,0,1:T(8,128)(2,1)} fusion(bf16[16,1024,256]{2,1,0:T(8,128)(2,1)} %all-gather.6.cloned.1.call-done, f32[256]{0:T(256)S(1)} %copy-done.16, f32[16,1024]{1,0:T(8,128)S(1)} %add_rsqrt_fusion, f32[16,1024]{1,0:T(8,128)S(1)} %broadcast_multiply_fusion, bf16[256,256]{1,0:T(8,128)(2,1)S(1)} %copy-done.11), kind=kOutput, calls=%fused_computation.36 | convolution fusion | flops 2172649472 | bytes 17040384 | tf_op jit(solution)/shard_map/dot_general | solution.py:64
  299.8 3.8 reshape.224
  303.6 2.8 copy.111
  306.4 4.1 reshape.202
  310.4 144.1 %while.23 = (s32[]{:T(128)}, f32[16,1,64,256]{3,2,0,1:T(8,128)}, f32[16,1,64,8]{2,3,1,0:T(8,128)S(1)}, bf16[16,1,1024,256]{3,2,0,1:T(8,128)(2,1)}, f32[16,1,1024...) while((s32[]{:T(128)}, f32[16,1,64,256]{3,2,0,1:T(8,128)}, ...), condition=%wide.region_11.12_spmd, body=%wide.region_8.0_spmd.sunk | while | flops 71827456 | bytes 13097581 | solution.py:86
  (301 shorter events, 194.3 us)
Async XLA Ops:
  7.2 452.0 %copy-start = (bf16[1024,256]{1,0:T(8,128)(2,1)S(1)}, bf16[1024,256]{1,0:T(8,128)(2,1)}, u32[]{:S(2)}) copy-start(bf16[1024,256]{1,0:T(8,128)(2,1)} %param.41) | copy-start | bytes 1572868
  7.2 142.7 %all-gather.6.cloned.1.call-start = ((), (), s32[]{:S(2)}) async-start(), calls=%async_computation.3 | async-start | bytes 8912896 | tf_op jit(solution)/shard_map/all_gather | solution.py:159
  7.9 182.1 %all-gather.4.cloned.1.call-start = ((), (), s32[]{:S(2)}) async-start(), calls=%async_computation.2 | async-start | bytes 2297856 | tf_op jit(solution)/shard_map/all_gather | solution.py:16
  149.9 5.8 %copy-start.1 = (bf16[16,1024,256]{2,1,0:T(8,128)(2,1)S(1)}, bf16[16,1024,256]{2,1,0:T(8,128)(2,1)}, u32[]{:S(2)}) copy-start(bf16[16,1024,256]{2,1,0:T(8,128)(2,1)} %all-gather.6.cloned.1.call-done) | copy-start | bytes 25165828
  155.7 4.9 %copy-start.14 = (bf16[256,32]{0,1:T(8,128)(2,1)S(1)}, bf16[256,32]{0,1:T(8,128)(2,1)}, u32[]{:S(2)}) copy-start(bf16[256,32]{0,1:T(8,128)(2,1)} %param.29) | copy-start | bytes 49156
  155.7 4.9 %copy-start.15 = (f32[256]{0:T(256)S(1)}, f32[256]{0:T(256)}, u32[]{:S(2)}) copy-start(f32[256]{0:T(256)} %param.27) | copy-start | bytes 3076
  173.4 14.9 %copy-start.3 = (bf16[16,64,256]{2,1,0:T(8,128)(2,1)S(1)}, bf16[16,64,256]{2,1,0:T(8,128)(2,1)}, u32[]{:S(2)}) copy-start(bf16[16,64,256]{2,1,0:T(8,128)(2,1)} %param.23) | copy-start | bytes 1572868
  173.4 14.9 %copy-start.9 = (bf16[256,256]{1,0:T(8,128)(2,1)S(1)}, bf16[256,256]{1,0:T(8,128)(2,1)}, u32[]{:S(2)}) copy-start(bf16[256,256]{1,0:T(8,128)(2,1)} %param.34) | copy-start | bytes 393220
  173.4 14.9 %copy-start.16 = (f32[256]{0:T(256)S(1)}, f32[256]{0:T(256)}, u32[]{:S(2)}) copy-start(f32[256]{0:T(256)} %param.33) | copy-start | bytes 3076
  182.8 21.7 %all-to-all-start = ((bf16[16,2,16896]{2,1,0:T(2,128)(2,1)}), bf16[16,2,16896]{2,1,0:T(2,128)(2,1)}, u32[]{:S(2)}, u32[]{:S(2)}) async-start(bf16[16,2,16896]{2,1,0:T(2,128)(2,1)} %reshape.221), calls=%async_computation | async-start | bytes 2162688 | tf_op jit(solution)/shard_map/all_to_all | solution.py:28
  190.0 1.6 slice-start
  234.1 2.0 copy-start.8
  243.8 2.0 copy-start.8
  253.5 2.0 copy-start.8
  263.2 2.0 copy-start.8
  267.3 4.3 copy-start.5
  267.3 4.3 copy-start.6
  273.6 7.5 %copy-start.10 = (bf16[256,256]{1,0:T(8,128)(2,1)S(1)}, bf16[256,256]{1,0:T(8,128)(2,1)}, u32[]{:S(2)}) copy-start(bf16[256,256]{1,0:T(8,128)(2,1)} %param.35) | copy-start | bytes 393220
  276.1 23.7 %all-to-all-start.1 = ((bf16[16,2,16384]{2,1,0:T(2,128)(2,1)}), bf16[16,2,16384]{2,1,0:T(2,128)(2,1)}, u32[]{:S(2)}, u32[]{:S(2)}) async-start(bf16[16,2,16384]{2,1,0:T(2,128)(2,1)} %reshape.223), calls=%async_computation.1 | async-start | bytes 2097152 | tf_op jit(solution)/shard_map/all_to_all | solution.py:41
  281.1 9.4 %copy-start.11 = (bf16[256,256]{1,0:T(8,128)(2,1)S(1)}, bf16[256,256]{1,0:T(8,128)(2,1)}, u32[]{:S(2)}) copy-start(bf16[256,256]{1,0:T(8,128)(2,1)} %param.36) | copy-start | bytes 393220
  454.5 1.7 copy-start.4
  454.5 1.7 copy-start.12
  456.3 2.9 copy-start.7
  456.3 2.9 copy-start.17
  (2 other events, 3.0 us)
Sparse Core Ops, SparseCore 0:
  10.6 139.2 all-gather.5
  152.2 37.7 all-gather.3
where the time goes:
time: 472 us; the launch traced here: 468 us
  local copies, waits for them, and re-layouts  147 us (31%)
  matrix products  114 us (24%)
  waiting for transfers between devices  107 us (23%)
  blocking collectives  38 us (8%)
  other arithmetic  29.6 us (6%)
  between operations  14.5 us (3%)
  starting transfers between devices  10.4 us (2%)
  loops' own time  8.26 us (2%)
    all_gather x1, waiting for transfers between devices, on_device(): lax.all_gather(alignment, 'seq', axis=1, tiled=True)  96.5 us
    dynamic_slice x80, local copies, waits for them, and re-layouts, in_blocks(): outputs = lax.map(function, shaped)  66.3 us
    all_gather x1, blocking collectives, on_device(): lax.all_gather(mask_local, 'seq', axis=1, tiled=True)  38 us
    dot_general x7, matrix products, project(): result = jnp.dot(flattened, weight, preferred_element_type=jnp.float32)  33.9 us
    dot_general x16, matrix products, head_scores(): jnp.einsum('sihd,sjhd->shij', query_rows.reshape(seq_block, row_count, he...  32.6 us
    unnamed x39, local copies, waits for them, and re-layouts  28.5 us
    dot_general x16, matrix products, head_weigh(): jnp.einsum('shij,sjhd->sihd', weights.astype(jnp.bfloat16), values.reshap...  24.3 us
    dot_general x4, matrix products, outer_rows(): lax.dot_general(left_piece, right_flat, (((0,), (0,)), ((), ())), preferr...  12.1 us
  transfers between devices with their start and end apart: 4, of which 3 were waited for; matrix products, arithmetic and copies ran while one was open for 14% of the time, Pallas kernels for 0%

commit v1 on v0

v1 whole, which is shorter than its diff:
```python
import functools

import jax
import jax.numpy as jnp
from jax import lax
from jax.experimental import pallas as pl
from jax.experimental.pallas import tpu as pltpu
from jax.sharding import PartitionSpec as P

EPSILON = 1e-05
MASKED = -1000000000.0
MESH = pl.DeviceIdType.MESH
F32, BF16 = jnp.float32, jnp.bfloat16
NN = (((1,), (0,)), ((), ()))
NT = (((1,), (1,)), ((), ()))
NZ = 8
HOPS = ((4, 3), (3, 4))


def mm(a, b, dims=NN):
    return lax.dot_general(a, b, dims, preferred_element_type=F32)


def kernel(
    left_in, right_in, kv_in, pair_in, align_in, w_ec, wb_t, pair_gain, wq, wg, wk, wv, wo, t_gain, w_up, w_down,
    expand, head_mask,
    pair_out, align_out,
    lg, rg, rt, bd, osc, inv_c, bias_own, bias_sib, bias_tab, kvg, kb, vb, mask_tab, sc_buf, p_buf, r_buf, tot_buf,
    gate_own, gate_far, gate_in,
    l_send, l_recv, t_sem, rx_sem, kx_sem, r_send, r_recv, k_send, k_recv, b_sem, pl_send, pl_recv, f_send, f_recv, g_sem,
):
    q = lax.axis_index("seq")
    r = lax.axis_index("res")
    z, x_hi = q // 2, q % 2
    core = r % 2
    y = (r // 2) % 4
    x_lo = r // 8
    x = x_hi * 2 + x_lo
    kt = r // 2
    mate_q = q + 1 - 2 * x_hi
    sib_r = r + 1 - 2 * core
    up_q = ((z + 1) % NZ) * 2 + x_hi
    down_q = ((z + NZ - 1) % NZ) * 2 + x_hi

    def dev(qq, rr):
        return {"seq": qq, "res": rr}

    def rcopy(src, dst, ss, rs, where):
        return pltpu.make_async_remote_copy(
            src_ref=src, dst_ref=dst, send_sem=ss, recv_sem=rs, device_id=where, device_id_type=MESH
        )

    barrier = pltpu.get_barrier_semaphore()

    def hello(where):
        pl.semaphore_signal(barrier, inc=1, device_id=where, device_id_type=MESH)

    for d in range(1, 16):
        hello(dev(q, (r + d) % 16))
    for d in range(8):
        hello(dev(mate_q, (r + 2 * d) % 16))
    hello(dev(up_q, r))
    hello(dev(down_q, r))

    @pl.when(q != r)
    def _():
        hello(dev(r, q))
        pl.semaphore_wait(barrier, 26)

    @pl.when(q == r)
    def _():
        pl.semaphore_wait(barrier, 25)

    def rows16(ref, at):
        return ref.at[pl.ds(pl.multiple_of(at * 16, 16), 16), :]

    own_q = pl.ds(pl.multiple_of(q * 16, 16), 16)
    sends = []

    trans = rcopy(right_in, rows16(rg, r), t_sem.at[0], t_sem.at[1], dev(r, q))

    @pl.when(q != r)
    def _():
        trans.start()

    @pl.when(q == r)
    def _():
        rg[own_q, :] = right_in[...]

    for d in range(1, 16):
        c = rcopy(left_in, rows16(lg, r), l_send.at[d], l_recv.at[d], dev(q, (r + d) % 16))
        c.start()
        sends.append(c)
    lg[pl.ds(pl.multiple_of(r * 16, 16), 16), :] = left_in[...]

    def right_item(zo, u):
        return rows16(rg, zo * 2 + u)

    def kv_item(zo, u):
        return kvg.at[zo * 2 + u]

    def side(a):
        return x_hi if a == 0 else 1 - x_hi

    def ring_send(item, ss, rs, a, d, k):
        zo = (z + NZ - k) % NZ if d == 0 else (z + k) % NZ
        ref = item(zo, side(a))
        c = rcopy(ref, ref, ss.at[a * 8 + d * 4 + k], rs.at[a * 8 + d * 4 + k], dev(up_q if d == 0 else down_q, r))
        c.start()
        sends.append(c)

    def ring_arrive(item, ss, rs, a, d, k):
        zo = (z + NZ - 1 - k) % NZ if d == 0 else (z + 1 + k) % NZ
        ref = item(zo, side(a))
        rcopy(ref, ref, ss.at[a * 8 + d * 4 + k], rs.at[a * 8 + d * 4 + k], dev(up_q if d == 0 else down_q, r)).wait_recv()
        return zo * 2 + side(a)

    def ring_stage(item, ss, rs, k):
        arrived = []
        for a in range(2):
            for d in range(2):
                if k - 1 < HOPS[a][d]:
                    arrived.append(ring_arrive(item, ss, rs, a, d, k - 1))
                    if k < HOPS[a][d]:
                        ring_send(item, ss, rs, a, d, k)
        return arrived

    right_ring = functools.partial(ring_stage, right_item, r_send, r_recv)
    kv_ring = functools.partial(ring_stage, kv_item, k_send, k_recv)

    kx = rcopy(kv_in.at[1 - x_hi], kvg.at[q], kx_sem.at[0], kx_sem.at[1], dev(mate_q, r))
    kx.start()
    sends.append(kx)
    kvg[q] = kv_in[x_hi]
    for d in range(2):
        ring_send(kv_item, k_send, k_recv, 0, d, 0)

    def fill(e, carry):
        blk = w_ec[pl.ds(pl.multiple_of(e * 32, 32), 32), :]
        none = jnp.zeros_like(blk)
        for i in range(4):
            bd[pl.ds(pl.multiple_of(e * 128 + i * 32, 32), 32), :] = jnp.concatenate(
                [blk if i == n else none for n in range(4)], axis=1
            )
        return carry

    @pl.when(q != r)
    def _():
        rcopy(right_in, rows16(rg, q), t_sem.at[0], t_sem.at[1], dev(r, q)).wait_recv()

    for d in range(2):
        ring_send(right_item, r_send, r_recv, 0, d, 0)
    rx = rcopy(rows16(rg, q), rows16(rg, q), rx_sem.at[0], rx_sem.at[1], dev(mate_q, r))
    rx.start()
    sends.append(rx)
    lax.fori_loop(0, 32, fill, 0)
    rcopy(rows16(rg, q), rows16(rg, mate_q), rx_sem.at[0], rx_sem.at[1], dev(mate_q, r)).wait_recv()
    for d in range(2):
        ring_send(right_item, r_send, r_recv, 1, d, 0)

    rcopy(kv_in.at[0], kvg.at[mate_q], kx_sem.at[0], kx_sem.at[1], dev(mate_q, r)).wait_recv()
    for d in range(2):
        ring_send(kv_item, k_send, k_recv, 1, d, 0)

    def kv_proj(slot):
        at = pl.ds(pl.multiple_of(slot * 64, 64), 64)
        block = kvg[slot, pl.ds(0, 512), :]
        keys = mm(block, wk[...]).astype(BF16)
        values = mm(block, wv[...]).astype(BF16)
        for s in range(8):
            kb[s, at, :] = keys[s * 64 : s * 64 + 64]
            vb[s, at, :] = values[s * 64 : s * 64 + 64]

    right_ring(1)
    kv_proj(q)
    right_ring(2)
    kv_proj(mate_q)
    right_ring(3)
    right_ring(4)
    for d in range(1, 16):
        rcopy(left_in, rows16(lg, (r + 16 - d) % 16), l_send.at[d], l_recv.at[d], dev(q, (r + d) % 16)).wait_recv()
    arrived = kv_ring(1)

    counts = lax.dot_general(rg[:, 2048:2176], lg[:, 2048:2176], (((0,), (0,)), ((), ())), preferred_element_type=F32)
    inv_c[...] = 1.0 / jnp.maximum(counts[0:64], 1.0)
    for n in range(16):
        rt[n * 128 : n * 128 + 128, :] = rg[:, n * 128 : n * 128 + 128].T
    lane = lax.broadcasted_iota(jnp.int32, (64, 128), 1)
    lane8 = lax.broadcasted_iota(jnp.int32, (8, 128), 1)
    own_half = lane8 // 64 == core
    first = core == 0

    def outer_block(t, carry):
        ib = (t + 2 * (1 - core)) % 4
        l_blk = lg[:, pl.ds(pl.multiple_of(ib * 512, 512), 512)]
        for ec in range(4):
            o = mm(rt[ec * 512 : ec * 512 + 512, :], l_blk).astype(BF16)
            for e in range(8):
                for g in range(4):
                    at = (ec * 8 + e) * 128
                    osc[g * 64 : g * 64 + 64, at : at + 128] = o[e * 64 : e * 64 + 64, g * 128 : g * 128 + 128]
        res = mm(osc[...], bd[...])
        for g in range(4):
            norms = []
            for n in range(4):
                i = ib * 16 + g * 4 + n
                scale = jnp.sum(jnp.where(lane == i, inv_c[...], 0.0), axis=1, keepdims=True)
                val = pair_in[i] + res[g * 64 : g * 64 + 64, n * 128 : n * 128 + 128] * scale
                pair_out[i] = val
                cen = val - jnp.mean(val, -1, keepdims=True)
                spread = jnp.mean(cen * cen, -1, keepdims=True)
                norms.append((cen * lax.rsqrt(spread + EPSILON) * pair_gain[...]).astype(BF16))
            b_t = mm(wb_t[...], jnp.concatenate(norms, axis=0), NT)
            tiles = []
            for n in range(2):
                tile = b_t[0:8, n * 128 : n * 128 + 128]
                turned = pltpu.roll(tile, 64, 1)
                tiles.append(jnp.where(own_half, jnp.where(first, tile, turned), 0.0))
                tiles.append(jnp.where(own_half, jnp.where(first, turned, tile), 0.0))
            bias_own[pl.ds(pl.multiple_of(ib * 128 + g * 32, 32), 32), :] = jnp.concatenate(tiles, axis=0).astype(BF16)
        return carry

    half = pl.ds(pl.multiple_of(core * 256, 256), 256)
    far_half = pl.ds(pl.multiple_of((1 - core) * 256, 256), 256)
    lax.fori_loop(0, 2, outer_block, 0)
    sib = rcopy(bias_own.at[far_half, :], bias_sib, b_sem.at[0], b_sem.at[1], dev(q, sib_r))
    sib.start()
    sends.append(sib)
    for slot in arrived:
        kv_proj(slot)
    lax.fori_loop(2, 4, outer_block, 0)
    sib.wait_recv()
    bias_tab[x_hi, kt, half, :] = bias_own[half, :] + bias_sib[...]

    def tab(xx, yy):
        return bias_tab.at[xx // 2, (xx % 2) * 4 + yy, half, :]

    def tab_far(xx, yy):
        return bias_tab.at[xx // 2, (xx % 2) * 4 + yy, far_half, :]

    for d in range(1, 16):
        xx, yy = (x + d // 4) % 4, (y + d % 4) % 4
        where = dev(z * 2 + xx // 2, (xx % 2) * 8 + yy * 2 + core)
        c = rcopy(tab(x, y), tab(x, y), pl_send.at[d], pl_recv.at[d], where)
        c.start()
        sends.append(c)
    c = rcopy(tab(x, y), tab(x, y), f_send.at[0], f_recv.at[0], dev(q, sib_r))
    c.start()
    sends.append(c)
    arrived = kv_ring(2)
    for slot in arrived:
        kv_proj(slot)
    for d in range(1, 16):
        xx, yy = (x + 4 - d // 4) % 4, (y + 4 - d % 4) % 4
        got = tab(xx, yy)
        rcopy(got, got, pl_send.at[d], pl_recv.at[d], dev(q, sib_r)).wait_recv()
        c = rcopy(got, got, f_send.at[d], f_recv.at[d], dev(q, sib_r))
        c.start()
        sends.append(c)
    arrived = kv_ring(3)
    for slot in arrived:
        kv_proj(slot)
    for d in range(16):
        xx, yy = (x + 4 - d // 4) % 4, (y + 4 - d % 4) % 4
        got = tab_far(xx, yy)
        rcopy(got, got, f_send.at[d], f_recv.at[d], dev(q, sib_r)).wait_recv()
    arrived = kv_ring(4)
    for slot in arrived:
        kv_proj(slot)

    for n in range(8):
        live = kvg[2 * n, pl.ds(512, 16), 0:128].astype(F32) + kvg[2 * n + 1, pl.ds(512, 16), 0:128].astype(F32)
        mask_tab[:, n * 128 : n * 128 + 128] = jnp.where(live > 0.5, 0.0, MASKED)

    lane_head = lax.broadcasted_iota(jnp.int32, (64, 128), 1) // 32

    def by_head(ref, tile):
        out = ref[pl.ds(tile * 4, 64, stride=8), :]
        for h in range(1, 4):
            out = jnp.where(lane_head == h, ref[pl.ds(tile * 4 + h, 64, stride=8), :], out)
        return out

    def attend(v, dest):
        def one(s, carry):
            at = pl.ds(pl.multiple_of(s * 64, 64), 64)
            block = kvg[z * 2 + v, at, :]
            queries = (mm(block, wq[...]) * 32**-0.5).astype(BF16)
            gates = jax.nn.sigmoid(mm(block, wg[...]))
            spread_q = (mm(expand[...], queries) * head_mask[...]).astype(BF16)
            sc_buf[...] = mm(spread_q, kb[s], NT)
            m_row = mask_tab[pl.ds(s, 1), :]
            for rb in range(16):
                rows = pl.ds(rb * 32, 32)
                bias = jnp.concatenate([bias_tab[v, n, rows, :].astype(F32) for n in range(8)], axis=1)
                sc = sc_buf[rows, :] + bias + m_row
                w = jnp.exp(sc - jnp.max(sc, -1, keepdims=True))
                tot_buf[rows, :] = jnp.broadcast_to(jnp.sum(w, -1, keepdims=True), (32, 128))
                p_buf[rows, :] = w.astype(BF16)
            mixed = mm(p_buf[...], vb[s])
            for tile in range(2):
                r_buf[tile] = mixed[:, tile * 128 : tile * 128 + 128]
                num = by_head(r_buf.at[tile], tile)
                den = by_head(tot_buf, tile)
                dest[at, pl.ds(tile * 128, 128)] = (num / den * gates[:, tile * 128 : tile * 128 + 128]).astype(BF16)
            return carry

        lax.fori_loop(0, 8, one, 0)

    def finish(gated, which):
        def part(n, carry):
            at = pl.ds(pl.multiple_of(n * 256, 256), 256)
            after = align_in[which, at, :].astype(F32) + mm(gated[at, :], wo[...])
            cen = after - jnp.mean(after, -1, keepdims=True)
            spread = jnp.mean(cen * cen, -1, keepdims=True)
            norm = (cen * lax.rsqrt(spread + EPSILON) * t_gain[...]).astype(BF16)
            hidden = jnp.maximum(mm(norm, w_up[...]), 0.0).astype(BF16)
            align_out[which, at, :] = after + mm(hidden, w_down[...])
            return carry

        lax.fori_loop(0, 2, part, 0)

    attend(1 - x_hi, gate_far)
    back = rcopy(gate_far, gate_in, g_sem.at[0], g_sem.at[1], dev(mate_q, r))
    back.start()
    sends.append(back)
    attend(x_hi, gate_own)
    finish(gate_own, x_hi)
    back.wait_recv()
    finish(gate_in, 1 - x_hi)

    @pl.when(q != r)
    def _():
        trans.wait_send()

    for c in sends:
        c.wait_send()


def on_device(
    alignment, alignment_mask, residue_mask, pair_input, outer_gain, left_weight, right_weight, outer_weight, pair_gain,
    bias_weight, row_gain, query_weight, key_weight, value_weight, gate_weight, output_weight, transition_gain, up_weight,
    down_weight,
):
    q = lax.axis_index("seq")
    x_hi = q % 2
    live = alignment_mask * lax.dynamic_slice_in_dim(residue_mask, q * 64, 64)[None, :]
    live_f = live.astype(F32)
    live_b = live.astype(BF16)
    values = alignment.astype(F32)
    center = values - jnp.mean(values, -1, keepdims=True)
    spread = jnp.mean(center * center, -1, keepdims=True)
    norm = center * lax.rsqrt(spread + EPSILON)
    outer_norm = (norm * outer_gain).astype(BF16)
    row_norm = (norm * row_gain).astype(BF16)
    both = jnp.dot(
        outer_norm.reshape(1024, 256),
        jnp.concatenate([left_weight, right_weight], axis=1),
        preferred_element_type=F32,
    ).reshape(16, 64, 64)
    both = (both * live_f[..., None]).astype(BF16)
    flags = jnp.pad(live_b, ((0, 0), (0, 64)))
    left = jnp.concatenate([both[..., :32].reshape(16, 2048), flags], axis=1)
    right = jnp.concatenate([both[..., 32:].transpose(0, 2, 1).reshape(16, 2048), flags], axis=1)
    none = jnp.zeros_like(live_b)
    marks = jnp.where(x_hi == 0, jnp.concatenate([live_b, none], axis=1), jnp.concatenate([none, live_b], axis=1))
    marks = jnp.pad(marks.reshape(2, 8, 128), ((0, 0), (0, 8), (0, 128)))
    kv = jnp.concatenate([row_norm.reshape(2, 512, 256), marks], axis=1)
    w_ec = outer_weight.reshape(32, 32, 128).transpose(1, 0, 2).reshape(1024, 128)
    wb_t = jnp.pad(bias_weight.T, ((0, 8), (0, 0)))
    at = jnp.arange(512)
    expand = (at[:, None] // 8 == jnp.arange(64)[None, :]).astype(BF16)
    head_mask = (at[:, None] % 8 == jnp.arange(256)[None, :] // 32).astype(F32)

    vm = pl.BlockSpec(memory_space=pltpu.VMEM)
    dma, v = pltpu.SemaphoreType.DMA, pltpu.VMEM
    pair_out, align_out = pl.pallas_call(
        kernel,
        out_shape=(jax.ShapeDtypeStruct((64, 64, 128), F32), jax.ShapeDtypeStruct((2, 512, 256), F32)),
        in_specs=[vm] * 18,
        out_specs=(vm, vm),
        scratch_shapes=[
            v((256, 2176), BF16), v((256, 2176), BF16), v((2048, 256), BF16), v((4096, 512), BF16), v((256, 4096), BF16),
            v((64, 128), F32), v((512, 128), BF16), v((256, 128), BF16), v((2, 8, 512, 128), BF16),
            v((16, 528, 256), BF16), v((8, 1024, 256), BF16), v((8, 1024, 256), BF16), v((16, 1024), F32),
            v((512, 1024), F32), v((512, 1024), BF16), v((2, 512, 128), F32), v((512, 128), F32),
            v((512, 256), BF16), v((512, 256), BF16), v((512, 256), BF16),
            dma((16,)), dma((16,)), dma((2,)), dma((2,)), dma((2,)), dma((16,)), dma((16,)), dma((16,)), dma((16,)),
            dma((2,)), dma((16,)), dma((16,)), dma((16,)), dma((16,)), dma((2,)),
        ],
        compiler_params=pltpu.CompilerParams(collective_id=0, has_side_effects=True, vmem_limit_bytes=60 << 20),
    )(
        left, right, kv, pair_input, alignment.reshape(2, 512, 256), w_ec, wb_t, pair_gain.reshape(1, 128), query_weight,
        gate_weight, key_weight, value_weight, output_weight, transition_gain.reshape(1, 256), up_weight, down_weight,
        expand, head_mask,
    )
    return pair_out, align_out.reshape(16, 64, 256)


def solution(mesh):
    rep = P()
    in_specs = (P("res", "seq", None), P("res", "seq"), rep, P("seq", "res", None)) + (rep,) * 15
    out_specs = (P("seq", "res", None), P("res", "seq", None))
    return jax.shard_map(on_device, mesh=mesh, in_specs=in_specs, out_specs=out_specs, check_vma=False)
```

time: 472 us -> 142 us (0.30)
  the two profiles are of different devices: /device:TPU:1 before, /device:TPU:8 now
where the time goes in v1:
time: 142 us; the launch traced here: 141 us
  Pallas kernels  126 us (89%)
  local copies, waits for them, and re-layouts  7.8 us (5%)
  other arithmetic  6.34 us (4%)
    pallas_call x1, Pallas kernels, on_device(): pl.pallas_call(kernel, out_shape=(jax.ShapeDtypeStruct((64, 64, 128), F32...  126 us
    unnamed x18, local copies, waits for them, and re-layouts  4.26 us

profile of v1, /device:TPU:8, one launch (start us, length us, event | category | flops | bytes accessed | tf_op | source)
XLA Modules:
  0.0 141.3 jit_solution(16589129843490704449)
XLA Ops:
  0.6 0.0 copy-start
  0.6 0.0 copy-start.5
  0.7 0.0 copy-start.6
  0.7 0.8 dynamic_slice.3
  1.5 1.3 pad.16.wb_t
  2.8 1.2 convert_reduce_fusion
  4.1 1.4 %fusion.8 = f32[16,64]{1,0:T(8,128)S(1)} fusion(bf16[16,64,256]{2,1,0:T(8,128)(2,1)} %param.19, f32[16,64]{1,0:T(8,128)S(1)} %broadcast_multiply_fusion), kind=kLoop, calls=%fused_computation.12 | loop fusion | flops 1047552 | bytes 532480 | tf_op jit(solution)/shard_map/reduce_sum | solution.py:351
  5.5 0.1 select_bitcast_fusion
  5.6 0.8 fusion.14.expand
  6.4 0.0 copy-done.5
  6.4 0.5 fusion.2
  6.9 0.0 copy-start.2
  6.9 0.0 copy-start.4
  7.0 0.2 reshape.144
  7.2 0.2 copy.23
  7.3 0.3 reshape.143
  7.6 0.7 pad_maximum_fusion
  8.3 0.8 copy.24
  9.1 0.3 fusion.7
  9.4 0.8 fusion.9.kv_in
  10.3 0.9 compare_convert_fusion.head_mask
  11.2 125.9 %shard_map.194 = (f32[64,64,128]{2,1,0:T(8,128)}, f32[2,512,256]{2,1,0:T(8,128)}) custom-call(bf16[16,2176]{1,0:T(8,128)(2,1)} %get-tuple-element.13.left_in, bf16[16,2176]{1,0:T(8,128)(2,1)} %get-tuple-element.12.right_in, bf16[2,528,256]{2,1,0:T(8,128)(2,1)} %fusion.9.kv_in, f32[64,64,128]{2,1,0:T(8,128)} %pair_in.1, bf16[2,512,256]{2,1,0:T(8,128)(2,1)} %bitcast.17, ...), custom_call_target="tpu_custom_call" | custom-call | tf_op jit(solution)/shard_map/pallas_call | solution.py:376
  137.1 3.2 %copy.27 = f32[64,64,128]{2,1,0:T(8,128)} copy(f32[64,64,128]{2,1,0:T(8,128)} %get-tuple-element.16) | data formatting | bytes 4194304
  140.4 1.0 copy.28
  (17 shorter events, 0.1 us)
Async XLA Ops:
  0.6 5.8 %copy-start = (bf16[16,64,256]{2,1,0:T(8,128)(2,1)S(1)}, bf16[16,64,256]{2,1,0:T(8,128)(2,1)}, u32[]{:S(2)}) copy-start(bf16[16,64,256]{2,1,0:T(8,128)(2,1)} %param.19) | copy-start | bytes 1572868
  0.6 5.8 %copy-start.5 = (bf16[256,32]{0,1:T(8,128)(2,1)S(1)}, bf16[256,32]{0,1:T(8,128)(2,1)}, u32[]{:S(2)}) copy-start(bf16[256,32]{0,1:T(8,128)(2,1)} %param.25) | copy-start | bytes 49156
  0.7 5.7 %copy-start.6 = (bf16[256,32]{0,1:T(8,128)(2,1)S(1)}, bf16[256,32]{0,1:T(8,128)(2,1)}, u32[]{:S(2)}) copy-start(bf16[256,32]{0,1:T(8,128)(2,1)} %param.24) | copy-start | bytes 49156
  0.7 5.7 %copy-start.7 = (f32[256]{0:T(256)S(1)}, f32[256]{0:T(256)}, u32[]{:S(2)}) copy-start(f32[256]{0:T(256)} %param.23) | copy-start | bytes 3076
  0.7 4.8 %copy-start.3 = (s32[16,64]{1,0:T(8,128)S(1)}, s32[16,64]{1,0:T(8,128)}, u32[]{:S(2)}) copy-start(s32[16,64]{1,0:T(8,128)} %param.20) | copy-start | bytes 12292
  6.9 1.4 copy-start.2
  6.9 2.2 %copy-start.4 = (f32[256]{0:T(256)S(1)}, f32[256]{0:T(256)}, u32[]{:S(2)}) copy-start(f32[256]{0:T(256)} %param.29) | copy-start | bytes 3076
  137.1 3.3 %copy-start.1 = (f32[2,512,256]{2,1,0:T(8,128)S(1)}, f32[2,512,256]{2,1,0:T(8,128)}, u32[]{:S(2)}) copy-start(f32[2,512,256]{2,1,0:T(8,128)} %get-tuple-element.5) | copy-start | bytes 3145732

commit v2 on v1

--- a/solution.py
+++ b/solution.py
@@ -22,9 +22,11 @@
 
 
 def kernel(
-    left_in, right_in, kv_in, pair_in, align_in, w_ec, wb_t, pair_gain, wq, wg, wk, wv, wo, t_gain, w_up, w_down,
-    expand, head_mask,
-    pair_out, align_out,
+    align_in, a_mask, r_mask, o_gain, wl_t, wr_t, p_gain, wb_t, row_gain, t_gain,
+    pair_hbm, ow_hbm, wq_hbm, wk_hbm, wv_hbm, wg_hbm, wo_hbm, up_hbm, down_hbm,
+    pair_hbm_out, align_out,
+    left_in, right_in, kv_in, on, live_f, turn, pair_in, pair_out, w_bf, w_f32, wq, wk, wv, wg, wo, w_up, w_down,
+    expand, head_mask, in_sem,
     lg, rg, rt, bd, osc, inv_c, bias_own, bias_sib, bias_tab, kvg, kb, vb, mask_tab, sc_buf, p_buf, r_buf, tot_buf,
     gate_own, gate_far, gate_in,
     l_send, l_recv, t_sem, rx_sem, kx_sem, r_send, r_recv, k_send, k_recv, b_sem, pl_send, pl_recv, f_send, f_recv, g_sem,
@@ -65,6 +67,72 @@
     @pl.when(q != r)
     def _():
         hello(dev(r, q))
+
+    loads = [
+        pltpu.make_async_copy(src, dst, in_sem.at[n])
+        for n, (src, dst) in enumerate(
+            (
+                (ow_hbm, w_bf), (wk_hbm, wk), (wv_hbm, wv), (pair_hbm, pair_in), (wq_hbm, wq), (wg_hbm, wg), (wo_hbm, wo),
+                (up_hbm, w_up), (down_hbm, w_down),
+            )
+        )
+    ]
+    for c in loads:
+        c.start()
+
+    def iota(shape, dim):
+        return lax.broadcasted_iota(jnp.int32, shape, dim)
+
+    flag_row = r_mask[pl.ds(q // 2, 1), :].astype(F32)
+    flag_row = jnp.where(x_hi == 0, flag_row, pltpu.roll(flag_row, 64, 1))
+    live_f[...] = jnp.zeros_like(live_f)
+    live_f[:, 0:64] = a_mask[...].astype(F32) * flag_row[:, 0:64]
+    live = live_f[...]
+    live_b = live.astype(BF16)
+
+    def norms(n, carry):
+        at = pl.ds(pl.multiple_of(n * 256, 256), 256)
+        vals = align_in[n // 2, pl.ds(pl.multiple_of((n % 2) * 256, 256), 256), :].astype(F32)
+        cen = vals - jnp.mean(vals, -1, keepdims=True)
+        spread = jnp.mean(cen * cen, -1, keepdims=True)
+        norm = cen * lax.rsqrt(spread + EPSILON)
+        pick = (iota((256, 16), 0) // 64 + n * 4 == iota((256, 16), 1)).astype(F32).astype(BF16)
+        flags = mm(pick, live_b)
+        flag = jnp.sum(jnp.where(iota((256, 128), 0) % 64 == iota((256, 128), 1), flags, 0.0), -1, keepdims=True)
+        on[at, :] = (norm * o_gain[...] * flag).astype(BF16)
+        kv_in[n // 2, pl.ds(pl.multiple_of((n % 2) * 256, 256), 256), :] = (norm * row_gain[...]).astype(BF16)
+        return carry
+
+    lax.fori_loop(0, 4, norms, 0)
+    marks = jnp.where(x_hi == 0, live, pltpu.roll(live, 64, 1))
+    for h in range(2):
+        kv_in[h, pl.ds(512, 16), 0:128] = jnp.concatenate(
+            [marks[h * 8 : h * 8 + 8], jnp.zeros((8, 128), F32)], axis=0
+        ).astype(BF16)
+        kv_in[h, pl.ds(512, 16), 128:256] = jnp.zeros((16, 128), BF16)
+    r_t = mm(wr_t[...], on[...], NT)
+    for n in range(8):
+        tile = r_t[:, n * 128 : n * 128 + 128]
+        turn[n * 64 : n * 64 + 32, :] = tile
+        turn[n * 64 + 32 : n * 64 + 64, :] = pltpu.roll(tile, 64, 1)
+    low = iota((16, 128), 1) < 64
+    for n in range(16):
+        even = turn[pl.ds(2 * n, 16, stride=32), :]
+        odd = turn[pl.ds(2 * n + 1, 16, stride=32), :]
+        right_in[:, n * 128 : n * 128 + 128] = jnp.where(low, even, pltpu.roll(odd, 64, 1)).astype(BF16)
+    right_in[:, 2048:2176] = live_b
+    four = jnp.concatenate([wl_t[...]] * 4, axis=0)
+    l_all = mm(on[...], four, NT)
+    l_all = jnp.where(iota((1024, 128), 0) % 4 == iota((1024, 128), 1) // 32, l_all, 0.0).astype(BF16)
+    to, fro = iota((256, 1024), 0), iota((256, 1024), 1)
+    pick = ((fro // 64 == to % 16) & ((fro % 64) // 4 == to // 16)).astype(F32).astype(BF16)
+    l_rows = mm(pick, l_all).astype(BF16)
+    for n in range(16):
+        left_in[:, n * 128 : n * 128 + 128] = l_rows[n * 16 : n * 16 + 16]
+    left_in[:, 2048:2176] = live_b
+
+    @pl.when(q != r)
+    def _():
         pl.semaphore_wait(barrier, 26)
 
     @pl.when(q == r)
@@ -136,7 +204,7 @@
         ring_send(kv_item, k_send, k_recv, 0, d, 0)
 
     def fill(e, carry):
-        blk = w_ec[pl.ds(pl.multiple_of(e * 32, 32), 32), :]
+        blk = w_f32[pl.ds(e, 32, stride=32), :].astype(BF16)
         none = jnp.zeros_like(blk)
         for i in range(4):
             bd[pl.ds(pl.multiple_of(e * 128 + i * 32, 32), 32), :] = jnp.concatenate(
@@ -153,7 +221,13 @@
     rx = rcopy(rows16(rg, q), rows16(rg, q), rx_sem.at[0], rx_sem.at[1], dev(mate_q, r))
     rx.start()
     sends.append(rx)
+    loads[0].wait()
+    w_f32[...] = w_bf[...].astype(F32)
     lax.fori_loop(0, 32, fill, 0)
+    expand[...] = (iota((512, 64), 0) // 8 == iota((512, 64), 1)).astype(F32).astype(BF16)
+    head_mask[...] = (iota((512, 256), 0) % 8 == iota((512, 256), 1) // 32).astype(F32)
+    loads[1].wait()
+    loads[2].wait()
     rcopy(rows16(rg, q), rows16(rg, mate_q), rx_sem.at[0], rx_sem.at[1], dev(mate_q, r)).wait_recv()
     for d in range(2):
         ring_send(right_item, r_send, r_recv, 1, d, 0)
@@ -180,6 +254,8 @@
     for d in range(1, 16):
         rcopy(left_in, rows16(lg, (r + 16 - d) % 16), l_send.at[d], l_recv.at[d], dev(q, (r + d) % 16)).wait_recv()
     arrived = kv_ring(1)
+
+    loads[3].wait()
 
     counts = lax.dot_general(rg[:, 2048:2176], lg[:, 2048:2176], (((0,), (0,)), ((), ())), preferred_element_type=F32)
     inv_c[...] = 1.0 / jnp.maximum(counts[0:64], 1.0)
@@ -209,7 +285,7 @@
                 pair_out[i] = val
                 cen = val - jnp.mean(val, -1, keepdims=True)
                 spread = jnp.mean(cen * cen, -1, keepdims=True)
-                norms.append((cen * lax.rsqrt(spread + EPSILON) * pair_gain[...]).astype(BF16))
+                norms.append((cen * lax.rsqrt(spread + EPSILON) * p_gain[...]).astype(BF16))
             b_t = mm(wb_t[...], jnp.concatenate(norms, axis=0), NT)
             tiles = []
             for n in range(2):
@@ -229,6 +305,8 @@
     for slot in arrived:
         kv_proj(slot)
     lax.fori_loop(2, 4, outer_block, 0)
+    pair_back = pltpu.make_async_copy(pair_out, pair_hbm_out, in_sem.at[9])
+    pair_back.start()
     sib.wait_recv()
     bias_tab[x_hi, kt, half, :] = bias_own[half, :] + bias_sib[...]
 
@@ -280,31 +358,51 @@
             out = jnp.where(lane_head == h, ref[pl.ds(tile * 4 + h, 64, stride=8), :], out)
         return out
 
+    for c in loads[4:]:
+        c.wait()
+
     def attend(v, dest):
-        def one(s, carry):
-            at = pl.ds(pl.multiple_of(s * 64, 64), 64)
-            block = kvg[z * 2 + v, at, :]
-            queries = (mm(block, wq[...]) * 32**-0.5).astype(BF16)
-            gates = jax.nn.sigmoid(mm(block, wg[...]))
+        def rows_of(s):
+            return pl.ds(pl.multiple_of(s * 64, 64), 64)
+
+        def look(s, slot):
+            queries = (mm(kvg[z * 2 + v, rows_of(s), :], wq[...]) * 32**-0.5).astype(BF16)
             spread_q = (mm(expand[...], queries) * head_mask[...]).astype(BF16)
-            sc_buf[...] = mm(spread_q, kb[s], NT)
+            sc_buf[slot] = mm(spread_q, kb[s], NT)
+
+        def weigh(s, slot):
             m_row = mask_tab[pl.ds(s, 1), :]
             for rb in range(16):
                 rows = pl.ds(rb * 32, 32)
                 bias = jnp.concatenate([bias_tab[v, n, rows, :].astype(F32) for n in range(8)], axis=1)
-                sc = sc_buf[rows, :] + bias + m_row
+                sc = sc_buf[slot, rows, :] + bias + m_row
                 w = jnp.exp(sc - jnp.max(sc, -1, keepdims=True))
-                tot_buf[rows, :] = jnp.broadcast_to(jnp.sum(w, -1, keepdims=True), (32, 128))
-                p_buf[rows, :] = w.astype(BF16)
-            mixed = mm(p_buf[...], vb[s])
+                tot_buf[slot, rows, :] = jnp.broadcast_to(jnp.sum(w, -1, keepdims=True), (32, 128))
+                p_buf[slot, rows, :] = w.astype(BF16)
+
+        def mix(s, slot):
+            gates = jax.nn.sigmoid(mm(kvg[z * 2 + v, rows_of(s), :], wg[...]))
+            mixed = mm(p_buf[slot], vb[s])
             for tile in range(2):
-                r_buf[tile] = mixed[:, tile * 128 : tile * 128 + 128]
-                num = by_head(r_buf.at[tile], tile)
-                den = by_head(tot_buf, tile)
-                dest[at, pl.ds(tile * 128, 128)] = (num / den * gates[:, tile * 128 : tile * 128 + 128]).astype(BF16)
+                r_buf[slot, tile] = mixed[:, tile * 128 : tile * 128 + 128]
+                num = by_head(r_buf.at[slot, tile], tile)
+                den = by_head(tot_buf.at[slot], tile)
+                dest[rows_of(s), pl.ds(tile * 128, 128)] = (
+                    num / den * gates[:, tile * 128 : tile * 128 + 128]
+                ).astype(BF16)
+
+        def two(n, carry):
+            s = n * 2
+            look(s + 1, 1)
+            weigh(s, 0)
+            mix(s, 0)
+            weigh(s + 1, 1)
+            look(lax.rem(s + 2, 8), 0)
+            mix(s + 1, 1)
             return carry
 
-        lax.fori_loop(0, 8, one, 0)
+        look(0, 0)
+        lax.fori_loop(0, 4, two, 0)
 
     def finish(gated, which):
         def part(n, carry):
@@ -334,6 +432,7 @@
 
     for c in sends:
         c.wait_send()
+    pair_back.wait()
 
 
 def on_device(
@@ -341,57 +440,32 @@
     bias_weight, row_gain, query_weight, key_weight, value_weight, gate_weight, output_weight, transition_gain, up_weight,
     down_weight,
 ):
-    q = lax.axis_index("seq")
-    x_hi = q % 2
-    live = alignment_mask * lax.dynamic_slice_in_dim(residue_mask, q * 64, 64)[None, :]
-    live_f = live.astype(F32)
-    live_b = live.astype(BF16)
-    values = alignment.astype(F32)
-    center = values - jnp.mean(values, -1, keepdims=True)
-    spread = jnp.mean(center * center, -1, keepdims=True)
-    norm = center * lax.rsqrt(spread + EPSILON)
-    outer_norm = (norm * outer_gain).astype(BF16)
-    row_norm = (norm * row_gain).astype(BF16)
-    both = jnp.dot(
-        outer_norm.reshape(1024, 256),
-        jnp.concatenate([left_weight, right_weight], axis=1),
-        preferred_element_type=F32,
-    ).reshape(16, 64, 64)
-    both = (both * live_f[..., None]).astype(BF16)
-    flags = jnp.pad(live_b, ((0, 0), (0, 64)))
-    left = jnp.concatenate([both[..., :32].reshape(16, 2048), flags], axis=1)
-    right = jnp.concatenate([both[..., 32:].transpose(0, 2, 1).reshape(16, 2048), flags], axis=1)
-    none = jnp.zeros_like(live_b)
-    marks = jnp.where(x_hi == 0, jnp.concatenate([live_b, none], axis=1), jnp.concatenate([none, live_b], axis=1))
-    marks = jnp.pad(marks.reshape(2, 8, 128), ((0, 0), (0, 8), (0, 128)))
-    kv = jnp.concatenate([row_norm.reshape(2, 512, 256), marks], axis=1)
-    w_ec = outer_weight.reshape(32, 32, 128).transpose(1, 0, 2).reshape(1024, 128)
-    wb_t = jnp.pad(bias_weight.T, ((0, 8), (0, 0)))
-    at = jnp.arange(512)
-    expand = (at[:, None] // 8 == jnp.arange(64)[None, :]).astype(BF16)
-    head_mask = (at[:, None] % 8 == jnp.arange(256)[None, :] // 32).astype(F32)
-
     vm = pl.BlockSpec(memory_space=pltpu.VMEM)
+    hbm = pl.BlockSpec(memory_space=pl.ANY)
     dma, v = pltpu.SemaphoreType.DMA, pltpu.VMEM
     pair_out, align_out = pl.pallas_call(
         kernel,
         out_shape=(jax.ShapeDtypeStruct((64, 64, 128), F32), jax.ShapeDtypeStruct((2, 512, 256), F32)),
-        in_specs=[vm] * 18,
-        out_specs=(vm, vm),
+        in_specs=[vm] * 10 + [hbm] * 9,
+        out_specs=(hbm, vm),
         scratch_shapes=[
+            v((16, 2176), BF16), v((16, 2176), BF16), v((2, 528, 256), BF16), v((1024, 256), BF16), v((16, 128), F32),
+            v((512, 128), F32), v((64, 64, 128), F32), v((64, 64, 128), F32), v((1024, 128), BF16), v((1024, 128), F32),
+            v((256, 256), BF16), v((256, 256), BF16), v((256, 256), BF16), v((256, 256), BF16), v((256, 256), BF16),
+            v((256, 1024), BF16), v((1024, 256), BF16), v((512, 64), BF16), v((512, 256), F32), dma((10,)),
             v((256, 2176), BF16), v((256, 2176), BF16), v((2048, 256), BF16), v((4096, 512), BF16), v((256, 4096), BF16),
             v((64, 128), F32), v((512, 128), BF16), v((256, 128), BF16), v((2, 8, 512, 128), BF16),
             v((16, 528, 256), BF16), v((8, 1024, 256), BF16), v((8, 1024, 256), BF16), v((16, 1024), F32),
-            v((512, 1024), F32), v((512, 1024), BF16), v((2, 512, 128), F32), v((512, 128), F32),
+            v((2, 512, 1024), F32), v((2, 512, 1024), BF16), v((2, 2, 512, 128), F32), v((2, 512, 128), F32),
             v((512, 256), BF16), v((512, 256), BF16), v((512, 256), BF16),
             dma((16,)), dma((16,)), dma((2,)), dma((2,)), dma((2,)), dma((16,)), dma((16,)), dma((16,)), dma((16,)),
             dma((2,)), dma((16,)), dma((16,)), dma((16,)), dma((16,)), dma((2,)),
         ],
         compiler_params=pltpu.CompilerParams(collective_id=0, has_side_effects=True, vmem_limit_bytes=60 << 20),
     )(
-        left, right, kv, pair_input, alignment.reshape(2, 512, 256), w_ec, wb_t, pair_gain.reshape(1, 128), query_weight,
-        gate_weight, key_weight, value_weight, output_weight, transition_gain.reshape(1, 256), up_weight, down_weight,
-        expand, head_mask,
+        alignment.reshape(2, 512, 256), alignment_mask, residue_mask.reshape(8, 128), outer_gain.reshape(1, 256), left_weight.T,
+        right_weight.T, pair_gain.reshape(1, 128), bias_weight.T, row_gain.reshape(1, 256), transition_gain.reshape(1, 256),
+        pair_input, outer_weight, query_weight, key_weight, value_weight, gate_weight, output_weight, up_weight, down_weight,
     )
     return pair_out, align_out.reshape(16, 64, 256)
 

time: 142 us -> 123 us (0.87)
  Pallas kernels: 126 us -> 118 us
  other arithmetic: 6.34 us -> 0 us
  local copies, waits for them, and re-layouts: 7.8 us -> 4.22 us
    pallas_call x1, Pallas kernels: 126 us -> 118 us  [on_device(): pl.pallas_call(kernel, out_shape=(jax.ShapeDtypeStruct((64, 64, 128), F32...]
    reduce_sum x2 -> x0, other arithmetic: 2.68 us -> none  [the longest x1 1.43 us: on_device(): spread = jnp.mean(center * center, -1, keepdims=True)]
    convert_element_type x4 -> x0, other arithmetic: 2.06 us -> none  [the longest x1 0.93 us: on_device(): head_mask = (at[:, None] % 8 == jnp.arange(256)[None, :] // 32).astype(F32)]
    concatenate x2 -> x0, other arithmetic: 1.5 us -> none  [the longest x1 0.83 us: on_device(): kv = jnp.concatenate([row_norm.reshape(2, 512, 256), marks], axis=1)]
    unnamed x18 -> x4, local copies, waits for them, and re-layouts: 4.26 us -> 4.22 us
where the time goes in v2:
time: 123 us
  Pallas kernels  118 us (96%)
  local copies, waits for them, and re-layouts  4.22 us (3%)
    pallas_call x1, Pallas kernels, on_device(): pl.pallas_call(kernel, out_shape=(jax.ShapeDtypeStruct((64, 64, 128), F32...  118 us
    unnamed x4, local copies, waits for them, and re-layouts  4.22 us

profile of v2, /device:TPU:8, one launch (start us, length us, event | category | flops | bytes accessed | tf_op | source)
XLA Modules:
  0.0 122.7 jit_solution(16584251401930428318)
XLA Ops:
  0.6 117.8 %shard_map.194 = (f32[64,64,128]{2,1,0:T(8,128)}, f32[2,512,256]{2,1,0:T(8,128)}) custom-call(bf16[2,512,256]{2,1,0:T(8,128)(2,1)} %bitcast.11, s32[16,64]{1,0:T(8,128)} %a_mask.1, s32[8,128]{1,0:T(8,128)} %bitcast.14, f32[1,256]{1,0:T(1,128)} %bitcast.16, bf16[32,256]{1,0:T(8,128)(2,1)} %bitcast.12, bf16[32,256]{1,0:T(8,128)(2,1)} %bitcast.13, ...), custom_call_target="tpu_custom_call" | custom-call | tf_op jit(solution)/shard_map/pallas_call | solution.py:446
  118.4 0.0 copy-start
  118.4 3.2 %copy.23 = f32[64,64,128]{2,1,0:T(8,128)} copy(f32[64,64,128]{2,1,0:T(8,128)} %get-tuple-element.8) | data formatting | bytes 4194304
  121.7 0.0 copy-done
  121.7 1.0 copy.24
Async XLA Ops:
  118.4 3.3 %copy-start = (f32[2,512,256]{2,1,0:T(8,128)S(1)}, f32[2,512,256]{2,1,0:T(8,128)}, u32[]{:S(2)}) copy-start(f32[2,512,256]{2,1,0:T(8,128)} %get-tuple-element.5) | copy-start | bytes 3145732

commit v3 on v2

--- a/solution.py
+++ b/solution.py
@@ -29,7 +29,8 @@
     expand, head_mask, in_sem,
     lg, rg, rt, bd, osc, inv_c, bias_own, bias_sib, bias_tab, kvg, kb, vb, mask_tab, sc_buf, p_buf, r_buf, tot_buf,
     gate_own, gate_far, gate_in,
-    l_send, l_recv, t_sem, rx_sem, kx_sem, r_send, r_recv, k_send, k_recv, b_sem, pl_send, pl_recv, f_send, f_recv, g_sem,
+    l_send, l_recv, t_sem, rx_send, rx_recv, kx_sem, r_send, r_recv, k_send, k_recv, b_sem, pl_send, pl_recv, f_send, f_recv,
+    g_sem,
 ):
     q = lax.axis_index("seq")
     r = lax.axis_index("res")
@@ -57,8 +58,9 @@
     def hello(where):
         pl.semaphore_signal(barrier, inc=1, device_id=where, device_id_type=MESH)
 
-    for d in range(1, 16):
-        hello(dev(q, (r + d) % 16))
+    for d in range(1, 8):
+        hello(dev(q, (r + 2 * d) % 16))
+    hello(dev(q, sib_r))
     for d in range(8):
         hello(dev(mate_q, (r + 2 * d) % 16))
     hello(dev(up_q, r))
@@ -100,16 +102,17 @@
         flags = mm(pick, live_b)
         flag = jnp.sum(jnp.where(iota((256, 128), 0) % 64 == iota((256, 128), 1), flags, 0.0), -1, keepdims=True)
         on[at, :] = (norm * o_gain[...] * flag).astype(BF16)
-        kv_in[n // 2, pl.ds(pl.multiple_of((n % 2) * 256, 256), 256), :] = (norm * row_gain[...]).astype(BF16)
+        kv_in[n // 2, pl.ds(pl.multiple_of((n % 2) * 272, 16), 256), :] = (norm * row_gain[...]).astype(BF16)
         return carry
 
     lax.fori_loop(0, 4, norms, 0)
     marks = jnp.where(x_hi == 0, live, pltpu.roll(live, 64, 1))
     for h in range(2):
-        kv_in[h, pl.ds(512, 16), 0:128] = jnp.concatenate(
-            [marks[h * 8 : h * 8 + 8], jnp.zeros((8, 128), F32)], axis=0
-        ).astype(BF16)
-        kv_in[h, pl.ds(512, 16), 128:256] = jnp.zeros((16, 128), BF16)
+        for g in range(2):
+            kv_in[h, pl.ds(g * 272 + 256, 16), 0:128] = jnp.concatenate(
+                [marks[h * 8 : h * 8 + 8], jnp.zeros((8, 128), F32)], axis=0
+            ).astype(BF16)
+            kv_in[h, pl.ds(g * 272 + 256, 16), 128:256] = jnp.zeros((16, 128), BF16)
     r_t = mm(wr_t[...], on[...], NT)
     for n in range(8):
         tile = r_t[:, n * 128 : n * 128 + 128]
@@ -133,11 +136,11 @@
 
     @pl.when(q != r)
     def _():
-        pl.semaphore_wait(barrier, 26)
+        pl.semaphore_wait(barrier, 19)
 
     @pl.when(q == r)
     def _():
-        pl.semaphore_wait(barrier, 25)
+        pl.semaphore_wait(barrier, 18)
 
     def rows16(ref, at):
         return ref.at[pl.ds(pl.multiple_of(at * 16, 16), 16), :]
@@ -145,63 +148,92 @@
     own_q = pl.ds(pl.multiple_of(q * 16, 16), 16)
     sends = []
 
-    trans = rcopy(right_in, rows16(rg, r), t_sem.at[0], t_sem.at[1], dev(r, q))
-
-    @pl.when(q != r)
-    def _():
-        trans.start()
-
-    @pl.when(q == r)
-    def _():
-        rg[own_q, :] = right_in[...]
-
-    for d in range(1, 16):
-        c = rcopy(left_in, rows16(lg, r), l_send.at[d], l_recv.at[d], dev(q, (r + d) % 16))
+    def go(c):
         c.start()
         sends.append(c)
-    lg[pl.ds(pl.multiple_of(r * 16, 16), 16), :] = left_in[...]
-
-    def right_item(zo, u):
-        return rows16(rg, zo * 2 + u)
-
-    def kv_item(zo, u):
-        return kvg.at[zo * 2 + u]
+
+    trans = rcopy(right_in, rows16(rg, r), t_sem.at[0], t_sem.at[1], dev(r, q))
+
+    @pl.when(q != r)
+    def _():
+        trans.start()
+
+    @pl.when(q == r)
+    def _():
+        rg[own_q, :] = right_in[...]
+
+    def ring_from(d, k):
+        return (z + NZ - 1 - k) % NZ if d == 0 else (z + 1 + k) % NZ
+
+    def ring_to(d, k):
+        return (z + NZ - k) % NZ if d == 0 else (z + k) % NZ
+
+    def ring_dev(d):
+        return dev(up_q if d == 0 else down_q, r)
 
     def side(a):
         return x_hi if a == 0 else 1 - x_hi
 
-    def ring_send(item, ss, rs, a, d, k):
-        zo = (z + NZ - k) % NZ if d == 0 else (z + k) % NZ
-        ref = item(zo, side(a))
-        c = rcopy(ref, ref, ss.at[a * 8 + d * 4 + k], rs.at[a * 8 + d * 4 + k], dev(up_q if d == 0 else down_q, r))
-        c.start()
-        sends.append(c)
-
-    def ring_arrive(item, ss, rs, a, d, k):
-        zo = (z + NZ - 1 - k) % NZ if d == 0 else (z + 1 + k) % NZ
-        ref = item(zo, side(a))
-        rcopy(ref, ref, ss.at[a * 8 + d * 4 + k], rs.at[a * 8 + d * 4 + k], dev(up_q if d == 0 else down_q, r)).wait_recv()
-        return zo * 2 + side(a)
-
-    def ring_stage(item, ss, rs, k):
-        arrived = []
-        for a in range(2):
-            for d in range(2):
-                if k - 1 < HOPS[a][d]:
-                    arrived.append(ring_arrive(item, ss, rs, a, d, k - 1))
-                    if k < HOPS[a][d]:
-                        ring_send(item, ss, rs, a, d, k)
-        return arrived
-
-    right_ring = functools.partial(ring_stage, right_item, r_send, r_recv)
-    kv_ring = functools.partial(ring_stage, kv_item, k_send, k_recv)
-
-    kx = rcopy(kv_in.at[1 - x_hi], kvg.at[q], kx_sem.at[0], kx_sem.at[1], dev(mate_q, r))
-    kx.start()
-    sends.append(kx)
+    def kv_copy(zo, g, a, d, k):
+        ref = kvg.at[zo * 2 + side(a), pl.ds(g * 272, 272), :]
+        n = g * 16 + a * 8 + d * 4 + k
+        return rcopy(ref, ref, k_send.at[n], k_recv.at[n], ring_dev(d))
+
+    waiting = [[], []]
+
+    def kv_start(g, a):
+        for d in range(2):
+            go(kv_copy(ring_to(d, 0), g, a, d, 0))
+
+    def kv_stage(g, a, k):
+        for d in range(2):
+            if k - 1 < HOPS[a][d]:
+                kv_copy(ring_from(d, k - 1), g, a, d, k - 1).wait_recv()
+                waiting[g].append(ring_from(d, k - 1) * 2 + side(a))
+                if k < HOPS[a][d]:
+                    go(kv_copy(ring_to(d, k), g, a, d, k))
+
+    def right_copy(zo, d, k):
+        ref = rows16(rg, zo * 2 + x_hi)
+        return rcopy(ref, ref, r_send.at[d * 4 + k], r_recv.at[d * 4 + k], ring_dev(d))
+
+    def mate_copy(zo, n, u):
+        ref = rows16(rg, zo * 2 + u)
+        return rcopy(ref, ref, rx_send.at[n], rx_recv.at[n], dev(mate_q, r))
+
+    def right_stage(k):
+        for d in range(2):
+            if k - 1 < HOPS[0][d]:
+                zo = ring_from(d, k - 1)
+                right_copy(zo, d, k - 1).wait_recv()
+                if k < HOPS[0][d]:
+                    go(right_copy(zo, d, k))
+                go(mate_copy(zo, d * 4 + k, x_hi))
+
+    def kx_copy(g):
+        at = pl.ds(g * 272, 272)
+        return rcopy(kv_in.at[1 - x_hi, at, :], kvg.at[q, at, :], kx_sem.at[2 * g], kx_sem.at[2 * g + 1], dev(mate_q, r))
+
+    def kx_wait(g):
+        at = pl.ds(g * 272, 272)
+        rcopy(kv_in.at[0, at, :], kvg.at[mate_q, at, :], kx_sem.at[2 * g], kx_sem.at[2 * g + 1], dev(mate_q, r)).wait_recv()
+        waiting[g].append(mate_q)
+
+    def left_copy(d):
+        return rcopy(left_in, rows16(lg, r), l_send.at[d], l_recv.at[d], dev(q, (r + 2 * d) % 16))
+
+    def left_pass(d, rr):
+        ref = rows16(lg, rr)
+        return rcopy(ref, ref, l_send.at[8 + d], l_recv.at[8 + d], dev(q, sib_r))
+
     kvg[q] = kv_in[x_hi]
-    for d in range(2):
-        ring_send(kv_item, k_send, k_recv, 0, d, 0)
+    kv_start(0, 0)
+    lg[pl.ds(pl.multiple_of(r * 16, 16), 16), :] = left_in[...]
+    for d in range(1, 8):
+        go(left_copy(d))
+    go(left_pass(0, r))
+    go(kx_copy(0))
+    go(kx_copy(1))
 
     def fill(e, carry):
         blk = w_f32[pl.ds(e, 32, stride=32), :].astype(BF16)
@@ -217,10 +249,8 @@
         rcopy(right_in, rows16(rg, q), t_sem.at[0], t_sem.at[1], dev(r, q)).wait_recv()
 
     for d in range(2):
-        ring_send(right_item, r_send, r_recv, 0, d, 0)
-    rx = rcopy(rows16(rg, q), rows16(rg, q), rx_sem.at[0], rx_sem.at[1], dev(mate_q, r))
-    rx.start()
-    sends.append(rx)
+        go(right_copy(z, d, 0))
+    go(mate_copy(z, 0, x_hi))
     loads[0].wait()
     w_f32[...] = w_bf[...].astype(F32)
     lax.fori_loop(0, 32, fill, 0)
@@ -228,33 +258,46 @@
     head_mask[...] = (iota((512, 256), 0) % 8 == iota((512, 256), 1) // 32).astype(F32)
     loads[1].wait()
     loads[2].wait()
-    rcopy(rows16(rg, q), rows16(rg, mate_q), rx_sem.at[0], rx_sem.at[1], dev(mate_q, r)).wait_recv()
-    for d in range(2):
-        ring_send(right_item, r_send, r_recv, 1, d, 0)
-
-    rcopy(kv_in.at[0], kvg.at[mate_q], kx_sem.at[0], kx_sem.at[1], dev(mate_q, r)).wait_recv()
-    for d in range(2):
-        ring_send(kv_item, k_send, k_recv, 1, d, 0)
-
-    def kv_proj(slot):
+    waiting[0].append(q)
+    waiting[1].append(q)
+    kx_wait(0)
+    kv_start(0, 1)
+
+    def kv_proj(slot, g):
         at = pl.ds(pl.multiple_of(slot * 64, 64), 64)
-        block = kvg[slot, pl.ds(0, 512), :]
+        block = kvg[slot, pl.ds(g * 272, 256), :]
         keys = mm(block, wk[...]).astype(BF16)
         values = mm(block, wv[...]).astype(BF16)
-        for s in range(8):
-            kb[s, at, :] = keys[s * 64 : s * 64 + 64]
-            vb[s, at, :] = values[s * 64 : s * 64 + 64]
-
-    right_ring(1)
-    kv_proj(q)
-    right_ring(2)
-    kv_proj(mate_q)
-    right_ring(3)
-    right_ring(4)
-    for d in range(1, 16):
-        rcopy(left_in, rows16(lg, (r + 16 - d) % 16), l_send.at[d], l_recv.at[d], dev(q, (r + d) % 16)).wait_recv()
-    arrived = kv_ring(1)
-
+        for s in range(4):
+            kb[g * 4 + s, at, :] = keys[s * 64 : s * 64 + 64]
+            vb[g * 4 + s, at, :] = values[s * 64 : s * 64 + 64]
+
+    def flush(g):
+        for slot in waiting[g]:
+            kv_proj(slot, g)
+        waiting[g].clear()
+
+    right_stage(1)
+    kv_stage(0, 0, 1)
+    flush(0)
+    right_stage(2)
+    for d in range(1, 8):
+        rcopy(left_in, rows16(lg, (r + 16 - 2 * d) % 16), l_send.at[d], l_recv.at[d], dev(q, sib_r)).wait_recv()
+        go(left_pass(d, (r + 16 - 2 * d) % 16))
+    kv_stage(0, 1, 1)
+    right_stage(3)
+    kv_stage(0, 0, 2)
+    right_stage(4)
+    for d in range(8):
+        left_pass(d, (sib_r + 16 - 2 * d) % 16).wait_recv()
+    kv_stage(0, 1, 2)
+    mate_copy(z, 0, 1 - x_hi).wait_recv()
+    for d in range(2):
+        for k in range(HOPS[0][d]):
+            mate_copy(ring_from(d, k), d * 4 + k + 1, 1 - x_hi).wait_recv()
+    kv_stage(0, 0, 3)
+    kx_wait(1)
+    kv_start(1, 0)
     loads[3].wait()
 
     counts = lax.dot_general(rg[:, 2048:2176], lg[:, 2048:2176], (((0,), (0,)), ((), ())), preferred_element_type=F32)
@@ -267,7 +310,7 @@
     first = core == 0
 
     def outer_block(t, carry):
-        ib = (t + 2 * (1 - core)) % 4
+        ib = t // 2 + 2 * ((core + 1 + t) % 2)
         l_blk = lg[:, pl.ds(pl.multiple_of(ib * 512, 512), 512)]
         for ec in range(4):
             o = mm(rt[ec * 512 : ec * 512 + 512, :], l_blk).astype(BF16)
@@ -296,58 +339,56 @@
             bias_own[pl.ds(pl.multiple_of(ib * 128 + g * 32, 32), 32), :] = jnp.concatenate(tiles, axis=0).astype(BF16)
         return carry
 
-    half = pl.ds(pl.multiple_of(core * 256, 256), 256)
-    far_half = pl.ds(pl.multiple_of((1 - core) * 256, 256), 256)
-    lax.fori_loop(0, 2, outer_block, 0)
-    sib = rcopy(bias_own.at[far_half, :], bias_sib, b_sem.at[0], b_sem.at[1], dev(q, sib_r))
-    sib.start()
-    sends.append(sib)
-    for slot in arrived:
-        kv_proj(slot)
-    lax.fori_loop(2, 4, outer_block, 0)
+    def quarter(c, own):
+        return pl.ds(pl.multiple_of((2 * (core if own else 1 - core) + c) * 128, 128), 128)
+
+    def tab(xx, yy, c, own):
+        return bias_tab.at[xx // 2, (xx % 2) * 4 + yy, quarter(c, own), :]
+
+    def spread_bias(c):
+        at = pl.ds(c * 128, 128)
+        rcopy(bias_own.at[quarter(c, False), :], bias_sib.at[at, :], b_sem.at[2 * c], b_sem.at[2 * c + 1], dev(q, sib_r)).wait_recv()
+        bias_tab[x_hi, kt, quarter(c, True), :] = bias_own[quarter(c, True), :] + bias_sib[at, :]
+        own = tab(x, y, c, True)
+        for d in range(1, 16):
+            xx, yy = (x + d // 4) % 4, (y + d % 4) % 4
+            where = dev(z * 2 + xx // 2, (xx % 2) * 8 + yy * 2 + core)
+            go(rcopy(own, own, pl_send.at[c * 16 + d], pl_recv.at[c * 16 + d], where))
+        go(rcopy(own, own, f_send.at[c * 16], f_recv.at[c * 16], dev(q, sib_r)))
+
+    def pass_bias(c):
+        for d in range(1, 16):
+            got = tab((x + 4 - d // 4) % 4, (y + 4 - d % 4) % 4, c, True)
+            rcopy(got, got, pl_send.at[c * 16 + d], pl_recv.at[c * 16 + d], dev(q, sib_r)).wait_recv()
+            go(rcopy(got, got, f_send.at[c * 16 + d], f_recv.at[c * 16 + d], dev(q, sib_r)))
+
+    for c in range(2):
+        lax.fori_loop(2 * c, 2 * c + 1, outer_block, 0)
+        at = pl.ds(c * 128, 128)
+        go(rcopy(bias_own.at[quarter(c, False), :], bias_sib.at[at, :], b_sem.at[2 * c], b_sem.at[2 * c + 1], dev(q, sib_r)))
+        lax.fori_loop(2 * c + 1, 2 * c + 2, outer_block, 0)
+        spread_bias(c)
+        if c == 0:
+            kv_stage(0, 1, 3)
+            kv_start(1, 1)
+            kv_stage(0, 0, 4)
+            kv_stage(0, 1, 4)
+            kv_stage(1, 0, 1)
     pair_back = pltpu.make_async_copy(pair_out, pair_hbm_out, in_sem.at[9])
     pair_back.start()
-    sib.wait_recv()
-    bias_tab[x_hi, kt, half, :] = bias_own[half, :] + bias_sib[...]
-
-    def tab(xx, yy):
-        return bias_tab.at[xx // 2, (xx % 2) * 4 + yy, half, :]
-
-    def tab_far(xx, yy):
-        return bias_tab.at[xx // 2, (xx % 2) * 4 + yy, far_half, :]
-
-    for d in range(1, 16):
-        xx, yy = (x + d // 4) % 4, (y + d % 4) % 4
-        where = dev(z * 2 + xx // 2, (xx % 2) * 8 + yy * 2 + core)
-        c = rcopy(tab(x, y), tab(x, y), pl_send.at[d], pl_recv.at[d], where)
-        c.start()
-        sends.append(c)
-    c = rcopy(tab(x, y), tab(x, y), f_send.at[0], f_recv.at[0], dev(q, sib_r))
-    c.start()
-    sends.append(c)
-    arrived = kv_ring(2)
-    for slot in arrived:
-        kv_proj(slot)
-    for d in range(1, 16):
-        xx, yy = (x + 4 - d // 4) % 4, (y + 4 - d % 4) % 4
-        got = tab(xx, yy)
-        rcopy(got, got, pl_send.at[d], pl_recv.at[d], dev(q, sib_r)).wait_recv()
-        c = rcopy(got, got, f_send.at[d], f_recv.at[d], dev(q, sib_r))
-        c.start()
-        sends.append(c)
-    arrived = kv_ring(3)
-    for slot in arrived:
-        kv_proj(slot)
-    for d in range(16):
-        xx, yy = (x + 4 - d // 4) % 4, (y + 4 - d % 4) % 4
-        got = tab_far(xx, yy)
-        rcopy(got, got, f_send.at[d], f_recv.at[d], dev(q, sib_r)).wait_recv()
-    arrived = kv_ring(4)
-    for slot in arrived:
-        kv_proj(slot)
+    kv_stage(1, 1, 1)
+    flush(0)
+    pass_bias(0)
+    kv_stage(1, 0, 2)
+    pass_bias(1)
+    kv_stage(1, 1, 2)
+    for c in range(2):
+        for d in range(16):
+            got = tab((x + 4 - d // 4) % 4, (y + 4 - d % 4) % 4, c, False)
+            rcopy(got, got, f_send.at[c * 16 + d], f_recv.at[c * 16 + d], dev(q, sib_r)).wait_recv()
 
     for n in range(8):
-        live = kvg[2 * n, pl.ds(512, 16), 0:128].astype(F32) + kvg[2 * n + 1, pl.ds(512, 16), 0:128].astype(F32)
+        live = kvg[2 * n, pl.ds(256, 16), 0:128].astype(F32) + kvg[2 * n + 1, pl.ds(256, 16), 0:128].astype(F32)
         mask_tab[:, n * 128 : n * 128 + 128] = jnp.where(live > 0.5, 0.0, MASKED)
 
     lane_head = lax.broadcasted_iota(jnp.int32, (64, 128), 1) // 32
@@ -361,12 +402,15 @@
     for c in loads[4:]:
         c.wait()
 
-    def attend(v, dest):
+    def attend(v, g, dest):
         def rows_of(s):
             return pl.ds(pl.multiple_of(s * 64, 64), 64)
 
+        def cells(s):
+            return kvg[z * 2 + v, pl.ds(pl.multiple_of(s * 64 + g * 16, 16), 64), :]
+
         def look(s, slot):
-            queries = (mm(kvg[z * 2 + v, rows_of(s), :], wq[...]) * 32**-0.5).astype(BF16)
+            queries = (mm(cells(s), wq[...]) * 32**-0.5).astype(BF16)
             spread_q = (mm(expand[...], queries) * head_mask[...]).astype(BF16)
             sc_buf[slot] = mm(spread_q, kb[s], NT)
 
@@ -381,7 +425,7 @@
                 p_buf[slot, rows, :] = w.astype(BF16)
 
         def mix(s, slot):
-            gates = jax.nn.sigmoid(mm(kvg[z * 2 + v, rows_of(s), :], wg[...]))
+            gates = jax.nn.sigmoid(mm(cells(s), wg[...]))
             mixed = mm(p_buf[slot], vb[s])
             for tile in range(2):
                 r_buf[slot, tile] = mixed[:, tile * 128 : tile * 128 + 128]
@@ -392,17 +436,17 @@
                 ).astype(BF16)
 
         def two(n, carry):
-            s = n * 2
+            s = n * 2 + g * 4
             look(s + 1, 1)
             weigh(s, 0)
             mix(s, 0)
             weigh(s + 1, 1)
-            look(lax.rem(s + 2, 8), 0)
+            look(g * 4 + (n * 2 + 2) % 4, 0)
             mix(s + 1, 1)
             return carry
 
-        look(0, 0)
-        lax.fori_loop(0, 4, two, 0)
+        look(g * 4, 0)
+        lax.fori_loop(0, 2, two, 0)
 
     def finish(gated, which):
         def part(n, carry):
@@ -417,13 +461,25 @@
 
         lax.fori_loop(0, 2, part, 0)
 
-    attend(1 - x_hi, gate_far)
-    back = rcopy(gate_far, gate_in, g_sem.at[0], g_sem.at[1], dev(mate_q, r))
-    back.start()
-    sends.append(back)
-    attend(x_hi, gate_own)
+    def back(g):
+        at = pl.ds(g * 256, 256)
+        return rcopy(gate_far.at[at, :], gate_in.at[at, :], g_sem.at[2 * g], g_sem.at[2 * g + 1], dev(mate_q, r))
+
+    attend(1 - x_hi, 0, gate_far)
+    go(back(0))
+    kv_stage(1, 0, 3)
+    kv_stage(1, 1, 3)
+    flush(1)
+    attend(x_hi, 0, gate_own)
+    kv_stage(1, 0, 4)
+    kv_stage(1, 1, 4)
+    flush(1)
+    attend(1 - x_hi, 1, gate_far)
+    go(back(1))
+    attend(x_hi, 1, gate_own)
     finish(gate_own, x_hi)
-    back.wait_recv()
+    for g in range(2):
+        back(g).wait_recv()
     finish(gate_in, 1 - x_hi)
 
     @pl.when(q != r)
@@ -449,17 +505,17 @@
         in_specs=[vm] * 10 + [hbm] * 9,
         out_specs=(hbm, vm),
         scratch_shapes=[
-            v((16, 2176), BF16), v((16, 2176), BF16), v((2, 528, 256), BF16), v((1024, 256), BF16), v((16, 128), F32),
+            v((16, 2176), BF16), v((16, 2176), BF16), v((2, 544, 256), BF16), v((1024, 256), BF16), v((16, 128), F32),
             v((512, 128), F32), v((64, 64, 128), F32), v((64, 64, 128), F32), v((1024, 128), BF16), v((1024, 128), F32),
             v((256, 256), BF16), v((256, 256), BF16), v((256, 256), BF16), v((256, 256), BF16), v((256, 256), BF16),
             v((256, 1024), BF16), v((1024, 256), BF16), v((512, 64), BF16), v((512, 256), F32), dma((10,)),
             v((256, 2176), BF16), v((256, 2176), BF16), v((2048, 256), BF16), v((4096, 512), BF16), v((256, 4096), BF16),
             v((64, 128), F32), v((512, 128), BF16), v((256, 128), BF16), v((2, 8, 512, 128), BF16),
-            v((16, 528, 256), BF16), v((8, 1024, 256), BF16), v((8, 1024, 256), BF16), v((16, 1024), F32),
+            v((16, 544, 256), BF16), v((8, 1024, 256), BF16), v((8, 1024, 256), BF16), v((16, 1024), F32),
             v((2, 512, 1024), F32), v((2, 512, 1024), BF16), v((2, 2, 512, 128), F32), v((2, 512, 128), F32),
             v((512, 256), BF16), v((512, 256), BF16), v((512, 256), BF16),
-            dma((16,)), dma((16,)), dma((2,)), dma((2,)), dma((2,)), dma((16,)), dma((16,)), dma((16,)), dma((16,)),
-            dma((2,)), dma((16,)), dma((16,)), dma((16,)), dma((16,)), dma((2,)),
+            dma((16,)), dma((16,)), dma((2,)), dma((8,)), dma((8,)), dma((4,)), dma((8,)), dma((8,)), dma((32,)), dma((32,)),
+            dma((4,)), dma((32,)), dma((32,)), dma((32,)), dma((32,)), dma((4,)),
         ],
         compiler_params=pltpu.CompilerParams(collective_id=0, has_side_effects=True, vmem_limit_bytes=60 << 20),
     )(

time: 123 us -> 110 us (0.89)
  the two profiles are of different devices: /device:TPU:8 before, /device:TPU:1 now
where the time goes in v3:
time: 110 us
  Pallas kernels  105 us (95%)
  local copies, waits for them, and re-layouts  4.22 us (4%)
    pallas_call x1, Pallas kernels, on_device(): pl.pallas_call(kernel, out_shape=(jax.ShapeDtypeStruct((64, 64, 128), F32...  105 us
    unnamed x4, local copies, waits for them, and re-layouts  4.22 us

profile of v3, /device:TPU:1, one launch (start us, length us, event | category | flops | bytes accessed | tf_op | source)
XLA Modules:
  0.0 110.2 jit_solution(8783612109134610542)
XLA Ops:
  0.6 105.4 %shard_map.194 = (f32[64,64,128]{2,1,0:T(8,128)}, f32[2,512,256]{2,1,0:T(8,128)}) custom-call(bf16[2,512,256]{2,1,0:T(8,128)(2,1)} %bitcast.11, s32[16,64]{1,0:T(8,128)} %a_mask.1, s32[8,128]{1,0:T(8,128)} %bitcast.14, f32[1,256]{1,0:T(1,128)} %bitcast.16, bf16[32,256]{1,0:T(8,128)(2,1)} %bitcast.12, bf16[32,256]{1,0:T(8,128)(2,1)} %bitcast.13, ...), custom_call_target="tpu_custom_call" | custom-call | tf_op jit(solution)/shard_map/pallas_call | solution.py:502
  106.0 0.0 copy-start
  106.0 3.2 %copy.23 = f32[64,64,128]{2,1,0:T(8,128)} copy(f32[64,64,128]{2,1,0:T(8,128)} %get-tuple-element.8) | data formatting | bytes 4194304
  109.3 0.0 copy-done
  109.3 1.0 copy.24
Async XLA Ops:
  106.0 3.3 %copy-start = (f32[2,512,256]{2,1,0:T(8,128)S(1)}, f32[2,512,256]{2,1,0:T(8,128)}, u32[]{:S(2)}) copy-start(f32[2,512,256]{2,1,0:T(8,128)} %get-tuple-element.5) | copy-start | bytes 3145732

commit v4 on v3

--- a/solution.py
+++ b/solution.py
@@ -27,7 +27,7 @@
     pair_hbm_out, align_out,
     left_in, right_in, kv_in, on, live_f, turn, pair_in, pair_out, w_bf, w_f32, wq, wk, wv, wg, wo, w_up, w_down,
     expand, head_mask, in_sem,
-    lg, rg, rt, bd, osc, inv_c, bias_own, bias_sib, bias_tab, kvg, kb, vb, mask_tab, sc_buf, p_buf, r_buf, tot_buf,
+    lg, rg, rt, bd, osc, inv_c, bias_own, bias_sib, bias_tab, kvg, kb, vb, mask_tab, sc_buf, p_buf, r_buf, tot_buf, top_buf,
     gate_own, gate_far, gate_in,
     l_send, l_recv, t_sem, rx_send, rx_recv, kx_sem, r_send, r_recv, k_send, k_recv, b_sem, pl_send, pl_recv, f_send, f_recv,
     g_sem,
@@ -233,7 +233,6 @@
         go(left_copy(d))
     go(left_pass(0, r))
     go(kx_copy(0))
-    go(kx_copy(1))
 
     def fill(e, carry):
         blk = w_f32[pl.ds(e, 32, stride=32), :].astype(BF16)
@@ -279,25 +278,25 @@
 
     right_stage(1)
     kv_stage(0, 0, 1)
-    flush(0)
+    go(kx_copy(1))
     right_stage(2)
+    kv_stage(0, 1, 1)
+    right_stage(3)
     for d in range(1, 8):
         rcopy(left_in, rows16(lg, (r + 16 - 2 * d) % 16), l_send.at[d], l_recv.at[d], dev(q, sib_r)).wait_recv()
         go(left_pass(d, (r + 16 - 2 * d) % 16))
-    kv_stage(0, 1, 1)
-    right_stage(3)
     kv_stage(0, 0, 2)
     right_stage(4)
+    kv_start(1, 0)
     for d in range(8):
         left_pass(d, (sib_r + 16 - 2 * d) % 16).wait_recv()
-    kv_stage(0, 1, 2)
     mate_copy(z, 0, 1 - x_hi).wait_recv()
     for d in range(2):
         for k in range(HOPS[0][d]):
             mate_copy(ring_from(d, k), d * 4 + k + 1, 1 - x_hi).wait_recv()
-    kv_stage(0, 0, 3)
+    kv_stage(0, 1, 2)
     kx_wait(1)
-    kv_start(1, 0)
+    kv_start(1, 1)
     loads[3].wait()
 
     counts = lax.dot_general(rg[:, 2048:2176], lg[:, 2048:2176], (((0,), (0,)), ((), ())), preferred_element_type=F32)
@@ -324,8 +323,9 @@
             for n in range(4):
                 i = ib * 16 + g * 4 + n
                 scale = jnp.sum(jnp.where(lane == i, inv_c[...], 0.0), axis=1, keepdims=True)
-                val = pair_in[i] + res[g * 64 : g * 64 + 64, n * 128 : n * 128 + 128] * scale
-                pair_out[i] = val
+                update = res[g * 64 : g * 64 + 64, n * 128 : n * 128 + 128] * scale
+                pair_out[i] = update
+                val = pair_in[i] + update
                 cen = val - jnp.mean(val, -1, keepdims=True)
                 spread = jnp.mean(cen * cen, -1, keepdims=True)
                 norms.append((cen * lax.rsqrt(spread + EPSILON) * p_gain[...]).astype(BF16))
@@ -369,19 +369,20 @@
         lax.fori_loop(2 * c + 1, 2 * c + 2, outer_block, 0)
         spread_bias(c)
         if c == 0:
-            kv_stage(0, 1, 3)
-            kv_start(1, 1)
-            kv_stage(0, 0, 4)
-            kv_stage(0, 1, 4)
+            kv_stage(0, 0, 3)
             kv_stage(1, 0, 1)
     pair_back = pltpu.make_async_copy(pair_out, pair_hbm_out, in_sem.at[9])
     pair_back.start()
+    kv_stage(0, 1, 3)
     kv_stage(1, 1, 1)
-    flush(0)
     pass_bias(0)
     kv_stage(1, 0, 2)
+    kv_stage(0, 0, 4)
+    flush(0)
+    kv_stage(1, 1, 2)
     pass_bias(1)
-    kv_stage(1, 1, 2)
+    kv_stage(0, 1, 4)
+    flush(0)
     for c in range(2):
         for d in range(16):
             got = tab((x + 4 - d // 4) % 4, (y + 4 - d % 4) % 4, c, False)
@@ -412,17 +413,28 @@
         def look(s, slot):
             queries = (mm(cells(s), wq[...]) * 32**-0.5).astype(BF16)
             spread_q = (mm(expand[...], queries) * head_mask[...]).astype(BF16)
-            sc_buf[slot] = mm(spread_q, kb[s], NT)
-
-        def weigh(s, slot):
+            sc = mm(spread_q, kb[s], NT)
             m_row = mask_tab[pl.ds(s, 1), :]
             for rb in range(16):
                 rows = pl.ds(rb * 32, 32)
-                bias = jnp.concatenate([bias_tab[v, n, rows, :].astype(F32) for n in range(8)], axis=1)
-                sc = sc_buf[slot, rows, :] + bias + m_row
-                w = jnp.exp(sc - jnp.max(sc, -1, keepdims=True))
-                tot_buf[slot, rows, :] = jnp.broadcast_to(jnp.sum(w, -1, keepdims=True), (32, 128))
-                p_buf[slot, rows, :] = w.astype(BF16)
+                top = None
+                for n in range(8):
+                    part = sc[rb * 32 : rb * 32 + 32, n * 128 : n * 128 + 128] + bias_tab[v, n, rows, :].astype(F32)
+                    part = part + m_row[:, n * 128 : n * 128 + 128]
+                    sc_buf[slot, rows, n * 128 : n * 128 + 128] = part
+                    top = part if n == 0 else jnp.maximum(top, part)
+                top_buf[slot, rows, :] = jnp.broadcast_to(jnp.max(top, -1, keepdims=True), (32, 128))
+
+        def weigh(slot):
+            for rb in range(16):
+                rows = pl.ds(rb * 32, 32)
+                top = top_buf[slot, rows, :]
+                total = None
+                for n in range(8):
+                    w = jnp.exp(sc_buf[slot, rows, n * 128 : n * 128 + 128] - top)
+                    p_buf[slot, rows, n * 128 : n * 128 + 128] = w.astype(BF16)
+                    total = w if n == 0 else total + w
+                tot_buf[slot, rows, :] = jnp.broadcast_to(jnp.sum(total, -1, keepdims=True), (32, 128))
 
         def mix(s, slot):
             gates = jax.nn.sigmoid(mm(cells(s), wg[...]))
@@ -438,9 +450,9 @@
         def two(n, carry):
             s = n * 2 + g * 4
             look(s + 1, 1)
-            weigh(s, 0)
+            weigh(0)
             mix(s, 0)
-            weigh(s + 1, 1)
+            weigh(1)
             look(g * 4 + (n * 2 + 2) % 4, 0)
             mix(s + 1, 1)
             return carry
@@ -513,6 +525,7 @@
             v((64, 128), F32), v((512, 128), BF16), v((256, 128), BF16), v((2, 8, 512, 128), BF16),
             v((16, 544, 256), BF16), v((8, 1024, 256), BF16), v((8, 1024, 256), BF16), v((16, 1024), F32),
             v((2, 512, 1024), F32), v((2, 512, 1024), BF16), v((2, 2, 512, 128), F32), v((2, 512, 128), F32),
+            v((2, 512, 128), F32),
             v((512, 256), BF16), v((512, 256), BF16), v((512, 256), BF16),
             dma((16,)), dma((16,)), dma((2,)), dma((8,)), dma((8,)), dma((4,)), dma((8,)), dma((8,)), dma((32,)), dma((32,)),
             dma((4,)), dma((32,)), dma((32,)), dma((32,)), dma((32,)), dma((4,)),
@@ -523,7 +536,7 @@
         right_weight.T, pair_gain.reshape(1, 128), bias_weight.T, row_gain.reshape(1, 256), transition_gain.reshape(1, 256),
         pair_input, outer_weight, query_weight, key_weight, value_weight, gate_weight, output_weight, up_weight, down_weight,
     )
-    return pair_out, align_out.reshape(16, 64, 256)
+    return pair_input + pair_out, align_out.reshape(16, 64, 256)
 
 
 def solution(mesh):

time: 110 us -> 106 us (0.964)
  Pallas kernels: 105 us -> 100 us
  other arithmetic: 0 us -> 3.56 us
  local copies, waits for them, and re-layouts: 4.22 us -> 0.98 us
    pallas_call x1, Pallas kernels: 105 us -> 100 us  [on_device(): pl.pallas_call(kernel, out_shape=(jax.ShapeDtypeStruct((64, 64, 128), F32...]
    add x0 -> x1, other arithmetic: none -> 3.56 us  [on_device(): return (pair_input + pair_out, align_out.reshape(16, 64, 256))]
    unnamed x4 -> x5, local copies, waits for them, and re-layouts: 4.22 us -> 0.98 us
where the time goes in v4:
time: 106 us
  Pallas kernels  100 us (94%)
  other arithmetic  3.56 us (3%)
    pallas_call x1, Pallas kernels, on_device(): pl.pallas_call(kernel, out_shape=(jax.ShapeDtypeStruct((64, 64, 128), F32...  100 us
    add x1, other arithmetic, on_device(): return (pair_input + pair_out, align_out.reshape(16, 64, 256))  3.56 us

profile of v4, /device:TPU:1, one launch (start us, length us, event | category | flops | bytes accessed | tf_op | source)
XLA Modules:
  0.0 105.6 jit_solution(579566143296754038)
XLA Ops:
  0.6 0.0 copy-start
  0.6 100.4 %shard_map.194 = (f32[64,64,128]{2,1,0:T(8,128)}, f32[2,512,256]{2,1,0:T(8,128)}) custom-call(bf16[2,512,256]{2,1,0:T(8,128)(2,1)} %bitcast.11, s32[16,64]{1,0:T(8,128)} %a_mask.1, s32[8,128]{1,0:T(8,128)} %bitcast.14, f32[1,256]{1,0:T(1,128)} %bitcast.16, bf16[32,256]{1,0:T(8,128)(2,1)} %bitcast.12, bf16[32,256]{1,0:T(8,128)(2,1)} %bitcast.13, ...), custom_call_target="tpu_custom_call" | custom-call | tf_op jit(solution)/shard_map/pallas_call | solution.py:514
  101.1 0.0 copy-done
  101.1 0.0 copy-start.1
  101.1 3.6 %add.3 = f32[64,64,128]{2,1,0:T(8,128)} add(f32[64,64,128]{2,1,0:T(8,128)S(1)} %copy-done, f32[64,64,128]{2,1,0:T(8,128)} %get-tuple-element.4) | non-fusion elementwise | flops 524288 | bytes 6291456 | tf_op jit(solution)/shard_map/add | solution.py:539
  104.6 0.0 copy-done.1
  104.6 1.0 copy.22
Async XLA Ops:
  0.6 100.4 %copy-start = (f32[64,64,128]{2,1,0:T(8,128)S(1)}, f32[64,64,128]{2,1,0:T(8,128)}, u32[]{:S(2)}) copy-start(f32[64,64,128]{2,1,0:T(8,128)} %pair_hbm.1) | copy-start | bytes 6291460
  101.1 3.6 %copy-start.1 = (f32[2,512,256]{2,1,0:T(8,128)S(1)}, f32[2,512,256]{2,1,0:T(8,128)}, u32[]{:S(2)}) copy-start(f32[2,512,256]{2,1,0:T(8,128)} %get-tuple-element.5) | copy-start | bytes 3145732
